TPU v7x, 32 devices: a whole 2x2x4 slice. The times are simulated.
32 devices in a mesh: dist: 4 (over y, x), rows: 8 (over z, core).
Axes of the slice: x: 2, y: 2, z: 4, core: 2. Of those that a mesh axis runs over, the one named last changes fastest.
Arguments:
- volume: bfloat16 [128, 128, 2048], P('rows', None, 'dist'), may hold values from -6 to 6
- kernels: bfloat16 [128, 2, 128, 128], P('rows'), may hold values from -0.09375 to 0.09375
- targets: int32 [128, 2], P('rows'), may hold values from 0 to 7, all different within a row; in each aligned block of 16 rows (0 to 15, 16 to 31, ...) at most 8 rows name the same one
- contrast: bfloat16 [4, 8, 128, 2048], P('dist', 'rows'), may hold values from -6 to 6
- fresnel_numbers: float32 [4], P('dist'), may hold values from 0.4 to 1.6
Outputs:
- gradient: bfloat16 [128, 128, 2048], P('rows', None, 'dist')
Inputs may be any that keep to these rules, and one draw needn't show every extreme that they name: `targets`: each row names 2 different detector blocks; among the rows of one index of rows no detector block is named more than 8 times, and some block is named exactly 8 times.
All inputs are finite; a program needn't handle non-finite values.
Results may differ from a plain program's by a relative error of at most 0.0063.
Values may be sent and summed in bfloat16 or wider, within the bound.
No kernel may reach another device: no remote copies, remote signals or barrier semaphores. Data moves between devices by JAX's collectives and lax.ppermute only.
A program may use at most 128 MiB of HBM per device.

v0:
```python
import math

import jax
import jax.numpy as jnp
from jax import lax
from jax.sharding import PartitionSpec as P


def spectral_table(width):
    half = width // 2
    index_rows = lax.broadcasted_iota(jnp.int32, (width, half), 0)
    index_cols = lax.broadcasted_iota(jnp.int32, (width, half), 1) + 1
    turns = (index_rows * index_cols % width).astype(jnp.float32) * (2.0 * math.pi / width)
    return jnp.concatenate([jnp.cos(turns), jnp.sin(turns)], axis=1)


def spectral_weight(width, number):
    half = width // 2
    freq = (lax.iota(jnp.int32, half) + 1).astype(jnp.float32)
    factor = jnp.sin(jnp.pi * number * freq * freq / width)
    scaled = factor * jnp.where(freq < half, 2.0, 1.0) / width
    return jnp.concatenate([scaled, scaled])


def shards(volume, kernels, targets, contrast, fresnel_numbers):
    owners = lax.axis_size("rows")
    vblocks, blk, quarter = volume.shape
    top = kernels.shape[1]
    items = vblocks * top
    width = contrast.shape[-1]
    contrib = jnp.einsum("btij,bjw->btiw", kernels, volume, preferred_element_type=jnp.float32)
    contrib = contrib.astype(jnp.bfloat16).reshape(items, blk * quarter)
    flat = targets.reshape(items)
    capacity = max(2, 2 * items // owners)
    later = lax.broadcasted_iota(jnp.int32, (items, items), 0)
    before = lax.broadcasted_iota(jnp.int32, (items, items), 1)
    same = (flat[:, None] == flat[None, :]) & (before < later)
    rank = jnp.sum(same.astype(jnp.int32), axis=1)
    slot = flat * capacity + rank
    place = (
        slot[None, :] == lax.broadcasted_iota(jnp.int32, (owners * capacity, items), 0)
    ).astype(jnp.bfloat16)
    outgoing = jnp.dot(place, contrib, preferred_element_type=jnp.float32).astype(jnp.bfloat16)
    outgoing = outgoing.reshape(owners, capacity, blk, quarter)
    arrived = lax.all_to_all(outgoing, "rows", split_axis=0, concat_axis=0, tiled=True)
    per_owner = jnp.sum(arrived.astype(jnp.float32), axis=1).astype(jnp.bfloat16)
    projection = jnp.sum(per_owner.astype(jnp.float32), axis=0)
    table = spectral_table(width)
    weight = spectral_weight(width, fresnel_numbers[0])
    spectrum = jnp.dot(
        lax.all_gather(projection, "dist", axis=1, tiled=True),
        table,
        precision=lax.Precision.HIGHEST,
        preferred_element_type=jnp.float32,
    )

    def synthesize(coeffs):
        return lax.dot_general(
            coeffs * weight,
            table,
            (((1,), (1,)), ((), ())),
            precision=lax.Precision.HIGHEST,
            preferred_element_type=jnp.float32,
        )

    residual = -2.0 * synthesize(spectrum) - contrast[0, 0].astype(jnp.float32)
    analysed = jnp.dot(
        residual, table, precision=lax.Precision.HIGHEST, preferred_element_type=jnp.float32
    )
    term = -2.0 * synthesize(analysed)
    summed = lax.psum(term, "dist")
    own_cols = lax.dynamic_slice_in_dim(summed, lax.axis_index("dist") * quarter, quarter, 1)
    image_gradient = own_cols.astype(jnp.bfloat16)
    piece = lax.all_gather(image_gradient[None], "rows", axis=0, tiled=True)
    count = piece.shape[0]
    pick = (flat[:, None] == lax.broadcasted_iota(jnp.int32, (items, count), 1)).astype(
        jnp.bfloat16
    )
    gathered = jnp.dot(
        pick, piece.reshape(count, blk * quarter), preferred_element_type=jnp.float32
    )
    chosen = gathered.astype(jnp.bfloat16).reshape(vblocks, top, blk, quarter)
    grad = jnp.einsum("btij,btiw->bjw", kernels, chosen, preferred_element_type=jnp.float32)
    return grad.astype(jnp.bfloat16)


def solution(mesh):
    in_specs = (
        P("rows", None, "dist"),
        P("rows", None, None, None),
        P("rows", None),
        P("dist", "rows", None, None),
        P("dist"),
    )
    out_specs = P("rows", None, "dist")
    return jax.shard_map(shards, mesh=mesh, in_specs=in_specs, out_specs=out_specs, check_vma=False)
```

profile of v0, /device:TPU:0, one launch (start us, length us, event | category | flops | bytes accessed | tf_op | source)
XLA Modules:
  0.0 398.3 jit_solution(16857438083517022711)
XLA Ops:
  6.5 0.0 copy-start
  6.5 0.0 all-gather.4.cloned.1.call-start
  6.5 0.9 copy.12
  7.4 0.1 eq.33
  7.5 0.2 convert_reduce_fusion.1
  7.7 0.4 copy-done
  8.1 2.5 convolution_convert_fusion.2
  10.6 2.4 copy.18
  13.0 2.3 convolution_convert_fusion
  15.3 190.6 %all_to_all.5 = bf16[8,8,128,512]{3,1,2,0:T(8,128)(2,1)} all-to-all(bf16[8,8,128,512]{3,1,2,0:T(8,128)(2,1)S(1)} %bitcast.32), channel_id=1, replica_groups=mesh['dist'=4,'rows'=8] {'rows'}, dimensions={0} | all-to-all | bytes 16777216 | tf_op jit(solution)/shard_map/all_to_all | solution.py:45
  206.0 9.2 %reduce_sum.31 = bf16[8,128,512]{2,1,0:T(8,128)(2,1)S(1)} reduce(bf16[8,8,128,512]{3,1,2,0:T(8,128)(2,1)} %all_to_all.5, bf16[]{:T(256)} %constant.18.clone.1), dimensions={1}, to_apply=%region_1.0 | reduce | flops 3670016 | bytes 9437186 | tf_op jit(solution)/shard_map/reduce_sum | solution.py:46
  215.2 0.8 convert_reduce_fusion
  216.0 0.0 all-gather.4.cloned.1.call-update
  216.0 0.3 all-gather.6.cloned.1.call-start
  217.0 0.1 fusion.25
  217.0 34.4 %fusion.11 = (f32[2048,1024]{1,0:T(8,128)}, f32[2048,1024]{1,0:T(8,128)}) fusion(s32[1024]{0:T(1024)S(1)} %iota_add_fusion), kind=kLoop, calls=%fused_computation.18 | loop fusion | flops 29360128 | bytes 16781312 | tf_op jit(solution)/shard_map/cos | solution.py:14
  251.4 0.0 all-gather.4.cloned.1.call-done
  251.4 0.0 copy-start.2
  251.4 0.0 copy-start.4
  251.4 15.1 %fusion.12 = f32[128,2048]{1,0:T(8,128)S(1)} fusion(f32[128,2048]{1,0:T(8,128)} %all-gather.4.cloned.1.call-done, f32[2048,1024]{1,0:T(8,128)} %get-tuple-element.6, f32[2048,1024]{1,0:T(8,128)} %get-tuple-element.5, f32[2048]{0:T(1024)S(1)} %pad_maximum_fusion.15), kind=kOutput, calls=%fused_computation.20 | convolution fusion | flops 6446907392 | bytes 18882560 | tf_op jit(solution)/shard_map/dot_general | solution.py:50
  266.5 0.0 copy-done.2
  266.6 0.0 copy-done.4
  266.6 19.9 %fusion.16 = f32[128,2048]{1,0:T(8,128)S(1)} fusion(f32[128,2048]{1,0:T(8,128)S(1)} %fusion.12, f32[2048,1024]{1,0:T(8,128)} %get-tuple-element.6, f32[2048,1024]{1,0:T(8,128)S(1)} %copy-done.2, bf16[1,1,128,2048]{3,2,1,0:T(8,128)(2,1)S(1)} %copy-done.4), kind=kOutput, calls=%fused_computation.24 | convolution fusion | flops 6447431680 | bytes 19398656 | tf_op jit(solution)/shard_map/dot_general | solution.py:58
  286.5 11.0 %fusion.14 = f32[128,2048]{1,0:T(8,128)S(1)} fusion(f32[128,2048]{1,0:T(8,128)S(1)} %fusion.16, f32[2048,1024]{1,0:T(8,128)} %get-tuple-element.6, f32[2048,1024]{1,0:T(8,128)S(1)} %copy-done.2, f32[2048]{0:T(1024)S(1)} %pad_maximum_fusion.15), kind=kOutput, calls=%fused_computation.22 | convolution fusion | flops 6446907392 | bytes 18882560 | tf_op jit(solution)/shard_map/dot_general | solution.py:67
  297.5 20.1 %fusion.15 = f32[128,2048]{1,0:T(8,128)S(1)} fusion(f32[128,2048]{1,0:T(8,128)S(1)} %fusion.14, f32[2048,1024]{1,0:T(8,128)} %get-tuple-element.6, f32[2048,1024]{1,0:T(8,128)S(1)} %copy-done.2), kind=kOutput, calls=%fused_computation.23 | convolution fusion | flops 6446907392 | bytes 18874368 | tf_op jit(solution)/shard_map/dot_general | solution.py:58
  317.6 41.0 %all-reduce.1 = bf16[128,2048]{1,0:T(8,128)(2,1)S(1)} all-reduce(f32[128,2048]{1,0:T(8,128)S(1)} %fusion.15), channel_id=1, replica_groups=mesh['dist'=4,'rows'=8] {'dist'}, use_global_device_ids=true, to_apply=%region_3.4 | all-reduce | flops 262144 | bytes 1572864 | tf_op jit(solution)/shard_map/psum | solution.py:71
  358.6 0.0 copy-start.3
  358.6 0.7 dynamic-slice_convert_fusion
  359.3 0.0 all-gather.6.cloned.1.call-update
  359.3 20.7 %all-gather.6.cloned.1.call-done = bf16[1024,512]{1,0:T(8,128)(2,1)} async-done(((bf16[128,512]{1,0:T(8,128)(2,1)}), bf16[1024,512]{1,0:T(8,128)(2,1)}) %all-gather.6.cloned.1.call-update) | async-done | bytes 1048592 | tf_op jit(solution)/shard_map/all_gather | solution.py:74
  380.0 1.7 reshape.30
  381.7 1.3 convolution_convert_fusion.1
  383.0 0.0 copy-start.1
  383.0 1.5 copy.19
  384.6 0.0 copy-done.3
  384.6 2.8 fusion.18
  387.3 3.9 copy.14
  391.2 0.0 copy-done.1
  (3 shorter events, 0.0 us)
Async XLA Ops:
  6.5 1.6 copy-start
  6.5 244.9 %all-gather.4.cloned.1.call-start = ((), (), s32[]{:S(2)}) async-start(), calls=%async_computation.1 | async-start | bytes 1310720 | tf_op jit(solution)/shard_map/all_gather | solution.py:51
  216.0 164.0 %all-gather.6.cloned.1.call-start = ((), (), s32[]{:S(2)}) async-start(), calls=%async_computation.2 | async-start | bytes 1179648 | tf_op jit(solution)/shard_map/all_gather | solution.py:74
  251.4 15.1 %copy-start.2 = (f32[2048,1024]{1,0:T(8,128)S(1)}, f32[2048,1024]{1,0:T(8,128)}, u32[]{:S(2)}) copy-start(f32[2048,1024]{1,0:T(8,128)} %get-tuple-element.5) | copy-start | bytes 25165828
  251.4 15.1 %copy-start.4 = (bf16[1,1,128,2048]{3,2,1,0:T(8,128)(2,1)S(1)}, bf16[1,1,128,2048]{3,2,1,0:T(8,128)(2,1)}, u32[]{:S(2)}) copy-start(bf16[1,1,128,2048]{3,2,1,0:T(8,128)(2,1)} %param.8) | copy-start | bytes 1572868
  358.6 26.0 %copy-start.3 = (bf16[16,2,128,128]{3,2,1,0:T(8,128)(2,1)S(1)}, bf16[16,2,128,128]{3,2,1,0:T(8,128)(2,1)}, u32[]{:S(2)}) copy-start(bf16[16,2,128,128]{3,2,1,0:T(8,128)(2,1)} %param.6) | copy-start | bytes 3145732
  383.0 8.2 %copy-start.1 = (bf16[16,128,512]{2,1,0:T(8,128)(2,1)S(1)}, bf16[16,128,512]{2,1,0:T(8,128)(2,1)}, u32[]{:S(2)}) copy-start(bf16[16,128,512]{2,1,0:T(8,128)(2,1)} %param.5) | copy-start | bytes 6291460
Sparse Core Ops, SparseCore 0:
  216.2 25.1 all-gather.3
  359.4 20.5 all-gather.5
where the time goes:
time: 403 us; the launch traced here: 398 us
  blocking collectives  232 us (58%)
  matrix products  74.9 us (19%)
  other arithmetic  44.7 us (11%)
  waiting for transfers between devices  20.7 us (5%)
  between operations  14.4 us (4%)
  local copies, waits for them, and re-layouts  11.7 us (3%)
    all_to_all x1, blocking collectives, shards(): lax.all_to_all(outgoing, 'rows', split_axis=0, concat_axis=0, tiled=True)  191 us
    psum x1, blocking collectives, shards(): summed = lax.psum(term, 'dist')  41 us
    dot_general x2, matrix products, synthesize(): lax.dot_general(coeffs * weight, table, (((1,), (1,)), ((), ())), precisi...  40.1 us
    cos x1, other arithmetic, spectral_table(): return jnp.concatenate([jnp.cos(turns), jnp.sin(turns)], axis=1)  34.4 us
    all_gather x1, waiting for transfers between devices, shards(): piece = lax.all_gather(image_gradient[None], 'rows', axis=0, tiled=True)  20.7 us
    dot_general x1, matrix products, shards(): jnp.dot(lax.all_gather(projection, 'dist', axis=1, tiled=True), table, pr...  15.1 us
    dot_general x1, matrix products, shards(): jnp.dot(residual, table, precision=lax.Precision.HIGHEST, preferred_eleme...  11 us
    reduce_sum x1, other arithmetic, shards(): jnp.sum(arrived.astype(jnp.float32), axis=1).astype(jnp.bfloat16)  9.19 us
  transfers between devices with their start and end apart: 2, of which 1 were waited for; matrix products, arithmetic and copies ran while one was open for 9% of the time, Pallas kernels for 0%

commit v1 on v0

v1 whole, which is shorter than its diff:
```python
import functools
import math

import jax
import jax.numpy as jnp
from jax import lax
from jax.experimental import pallas as pl
from jax.experimental.pallas import tpu as pltpu
from jax.sharding import PartitionSpec as P

BF16 = jnp.bfloat16
F32 = jnp.float32
DEEP = 256


def whole(memory_space=pltpu.VMEM):
    return pl.BlockSpec(memory_space=memory_space)


def swap(x, axis, mask):
    size = lax.axis_size(axis)
    return lax.ppermute(x, axis, [(i, i ^ mask) for i in range(size)])


def cost(flops, nbytes):
    return pl.CostEstimate(flops=flops, bytes_accessed=nbytes, transcendentals=0)


def project_kernel(me_ref, targets_ref, kernels_ref, volume_ref, send_ref, keep_ref, acc):
    step = pl.program_id(0)
    group, blk, _ = volume_ref.shape
    top = kernels_ref.shape[1]
    half = send_ref.shape[0]

    @pl.when(step == 0)
    def _():
        acc[...] = jnp.zeros_like(acc)

    me = me_ref[0]
    for b in range(group):
        product = jnp.dot(
            kernels_ref[b].reshape(top * blk, blk), volume_ref[b], preferred_element_type=F32
        )
        product = product.astype(BF16).astype(F32)
        for t in range(top):
            rel = targets_ref[step * group + b, t] ^ me
            slot = (rel & 1) * half + (rel >> 1)
            acc[slot] += product[t * blk : (t + 1) * blk]

    @pl.when(step == pl.num_programs(0) - 1)
    def _():
        keep_ref[...] = acc[:half].astype(BF16)
        send_ref[...] = acc[half:].astype(BF16)


def project(me, targets, kernels, volume, owners):
    vblocks, blk, quarter = volume.shape
    top = kernels.shape[1]
    half = owners // 2
    group = 4
    out = jax.ShapeDtypeStruct((half, blk, quarter), BF16)
    return pl.pallas_call(
        project_kernel,
        out_shape=(out, out),
        grid_spec=pltpu.PrefetchScalarGridSpec(
            num_scalar_prefetch=2,
            grid=(vblocks // group,),
            in_specs=[
                pl.BlockSpec((group, top, blk, blk), lambda s, *_: (s, 0, 0, 0)),
                pl.BlockSpec((group, blk, quarter), lambda s, *_: (s, 0, 0)),
            ],
            out_specs=[
                pl.BlockSpec((half, blk, quarter), lambda s, *_: (0, 0, 0)),
                pl.BlockSpec((half, blk, quarter), lambda s, *_: (0, 0, 0)),
            ],
            scratch_shapes=[pltpu.VMEM((owners, blk, quarter), F32)],
        ),
        cost_estimate=cost(2 * vblocks * top * blk * blk * quarter, 4 * 2**20),
        name="project",
    )(me, targets, kernels, volume)


def pair_kernel(keep_ref, came_ref, own_ref, *out_refs):
    own_ref[...] = keep_ref[0].astype(F32) + came_ref[0].astype(F32)
    for k, ref in enumerate(out_refs):
        ref[...] = (keep_ref[k + 1].astype(F32) + came_ref[k + 1].astype(F32)).astype(BF16)


def pair_sum(keep, came):
    half, blk, quarter = keep.shape
    return pl.pallas_call(
        pair_kernel,
        out_shape=[jax.ShapeDtypeStruct((blk, quarter), F32)]
        + [jax.ShapeDtypeStruct((blk, quarter), BF16)] * (half - 1),
        in_specs=[whole()] * 2,
        out_specs=[whole()] * half,
        cost_estimate=cost(half * blk * quarter, 6 * half * blk * quarter),
        name="pair_sum",
    )(keep, came)


def total_kernel(own_ref, *refs):
    total_ref, rounded_ref = refs[-2:]
    total = own_ref[...]
    for ref in refs[:-2]:
        total += ref[...].astype(F32)
    total_ref[...] = total
    rounded_ref[...] = total.astype(BF16)


def total_sum(own, came):
    return pl.pallas_call(
        total_kernel,
        out_shape=(
            jax.ShapeDtypeStruct(own.shape, F32),
            jax.ShapeDtypeStruct(own.shape, BF16),
        ),
        in_specs=[whole()] * (1 + len(came)),
        out_specs=[whole()] * 2,
        cost_estimate=cost(own.size * len(came), 8 * own.size),
        name="total_sum",
    )(own, *came)


def spectra(numbers, own, width, long):
    short = width // long
    k1 = lax.broadcasted_iota(jnp.int32, (short, long), 0)
    k2 = lax.broadcasted_iota(jnp.int32, (short, long), 1)
    freq = k1 + short * k2
    freq = jnp.minimum(freq, width - freq).astype(F32)
    squares = jnp.zeros((short, long), F32)
    for number in numbers:
        factor = jnp.sin(jnp.pi * number * freq * freq / width)
        squares += factor * factor
    both = 4.0 * squares - 4.0 * len(numbers) / 2
    single = 2.0 * jnp.sin(jnp.pi * own * freq * freq / width)
    return jnp.concatenate([both, single], axis=0)


def table_kernel(width, spectra_ref, contrast_ref, me_ref, table_ref, *refs):
    u_refs, extended = refs[:-1], refs[-1]
    rows2, long = spectra_ref.shape
    short = rows2 // 2
    n_dist = len(u_refs)
    quarter = width // n_dist

    def turns(shape, period, scale=1):
        a = lax.broadcasted_iota(jnp.int32, shape, 0)
        b = lax.broadcasted_iota(jnp.int32, shape, 1)
        angle = (a * b % period).astype(F32) * (2.0 * math.pi / period)
        return jnp.cos(angle), jnp.sin(angle)

    def mm(a, b):
        return jnp.dot(a, b, precision=lax.Precision.HIGHEST, preferred_element_type=F32)

    long_c, long_s = turns((long, long), long)
    twist_c, twist_s = turns((short, long), width)
    short_c, short_s = turns((short, short), short)
    spec = spectra_ref[...]
    yc, ys = mm(spec, long_c), mm(spec, long_s)
    for which in range(2):
        rows = slice(which * short, (which + 1) * short)
        re = yc[rows] * twist_c - ys[rows] * twist_s
        im = yc[rows] * twist_s + ys[rows] * twist_c
        g = (mm(short_c, re) - mm(short_s, im)) * (1.0 / width)
        line = jnp.concatenate([g[i : i + 1] for i in range(short)], axis=1)
        spread = jnp.broadcast_to(line, (DEEP, width))
        matrix = pltpu.roll(spread, 0, 1, stride=1, stride_axis=0).astype(BF16)
        if which == 0:
            table_ref[:, :width] = matrix
            table_ref[:, width:] = matrix[:, :quarter]
        else:
            extended[:, :width] = matrix
            extended[:, width:] = matrix
    me = me_ref[0]
    for k, ref in enumerate(u_refs):
        at = (me ^ k) * quarter
        total = jnp.zeros(ref.shape, F32)
        for i in range(width // DEEP):
            start = pl.multiple_of(width - i * DEEP + at, 128)
            start = pl.multiple_of(lax.rem(start, width), 128)
            total += jnp.dot(
                contrast_ref[:, i * DEEP : (i + 1) * DEEP],
                extended[:, pl.ds(start, quarter)],
                preferred_element_type=F32,
            )
        ref[...] = total.astype(BF16)


def tables(spectrum, contrast, me, n_dist):
    blk, width = contrast.shape
    quarter = width // n_dist
    return pl.pallas_call(
        functools.partial(table_kernel, width),
        out_shape=[jax.ShapeDtypeStruct((DEEP, width + quarter), BF16)]
        + [jax.ShapeDtypeStruct((blk, quarter), BF16)] * n_dist,
        in_specs=[whole(), whole(), whole(pltpu.SMEM)],
        out_specs=[whole()] * (1 + n_dist),
        scratch_shapes=[pltpu.VMEM((DEEP, 2 * width), BF16)],
        cost_estimate=cost(2 * blk * width * width, 3 * 2**20),
        name="tables",
    )(spectrum, contrast, me)


def filter_kernel(n_dist, me_ref, own_ref, table_ref, *refs):
    parts, terms, out_ref = refs[:n_dist], refs[n_dist:-1], refs[-1]
    blk, quarter = own_ref.shape
    width = n_dist * quarter
    me = me_ref[0]
    total = (2.0 * n_dist) * own_ref[...]
    for ref in terms:
        total += ref[...].astype(F32)
    for k, ref in enumerate(parts):
        for h in range(quarter // DEEP):
            start = (me - (me ^ k)) * quarter - h * DEEP + width
            start = pl.multiple_of(lax.rem(start, width), 128)
            total += jnp.dot(
                ref[:, h * DEEP : (h + 1) * DEEP],
                table_ref[:, pl.ds(start, quarter)],
                preferred_element_type=F32,
            )
    out_ref[...] = total.astype(BF16)


def filtered(me, own, table, parts, terms):
    blk, quarter = own.shape
    n_dist = len(parts)
    return pl.pallas_call(
        functools.partial(filter_kernel, n_dist),
        out_shape=jax.ShapeDtypeStruct((blk, quarter), BF16),
        in_specs=[whole(pltpu.SMEM)] + [whole()] * (2 + len(parts) + len(terms)),
        out_specs=whole(),
        cost_estimate=cost(2 * blk * quarter * quarter * n_dist, 3 * 2**20),
        name="filter",
    )(me, own, table, *parts, *terms)


def back_kernel(owners, me_ref, targets_ref, kernels_ref, *refs):
    parts, out_ref, chosen = refs[:owners], refs[owners], refs[owners + 1]
    step = pl.program_id(0)
    group, blk, quarter = out_ref.shape
    top = kernels_ref.shape[1]

    @pl.when(step == 0)
    def _():
        for k, ref in enumerate(parts):
            chosen[k] = ref[...]

    me = me_ref[0]
    for b in range(group):
        picked = [chosen[targets_ref[step * group + b, t] ^ me] for t in range(top)]
        out_ref[b] = lax.dot_general(
            kernels_ref[b].reshape(top * blk, blk),
            jnp.concatenate(picked, axis=0),
            (((0,), (0,)), ((), ())),
            preferred_element_type=F32,
        ).astype(BF16)


def back(me, targets, kernels, parts):
    vblocks, top, blk, _ = kernels.shape
    owners = len(parts)
    quarter = parts[0].shape[1]
    group = 4
    return pl.pallas_call(
        functools.partial(back_kernel, owners),
        out_shape=jax.ShapeDtypeStruct((vblocks, blk, quarter), BF16),
        grid_spec=pltpu.PrefetchScalarGridSpec(
            num_scalar_prefetch=2,
            grid=(vblocks // group,),
            in_specs=[pl.BlockSpec((group, top, blk, blk), lambda s, *_: (s, 0, 0, 0))]
            + [pl.BlockSpec((blk, quarter), lambda s, *_: (0, 0))] * owners,
            out_specs=pl.BlockSpec((group, blk, quarter), lambda s, *_: (s, 0, 0)),
            scratch_shapes=[pltpu.VMEM((owners, blk, quarter), BF16)],
        ),
        cost_estimate=cost(2 * vblocks * top * blk * blk * quarter, 4 * 2**20),
        name="back",
    )(me, targets, kernels, *parts)


def shards(volume, kernels, targets, contrast, fresnel_numbers):
    owners, n_dist = lax.axis_size("rows"), lax.axis_size("dist")
    me_rows = lax.axis_index("rows").astype(jnp.int32).reshape(1)
    me_dist = lax.axis_index("dist").astype(jnp.int32).reshape(1)
    half = owners // 2
    width = contrast.shape[-1]

    send, keep = project(me_rows, targets, kernels, volume, owners)
    came = swap(send, "rows", 1)
    own, *outgoing = pair_sum(keep, came)
    arrived = [swap(x, "rows", 2 * (k + 1)) for k, x in enumerate(outgoing)]

    numbers = [fresnel_numbers] + [swap(fresnel_numbers, "dist", k) for k in range(1, n_dist)]
    spectrum = spectra([x[0] for x in numbers], fresnel_numbers[0], width, 128)
    table, *terms = tables(spectrum, contrast[0, 0], me_dist, n_dist)
    terms = [terms[0]] + [swap(terms[k], "dist", k) for k in range(1, n_dist)]

    total, rounded = total_sum(own, arrived)
    parts = [rounded] + [swap(rounded, "dist", k) for k in range(1, n_dist)]
    image = filtered(me_dist, total, table, parts, terms)

    pieces = []
    for k in range(half):
        piece = image if k == 0 else swap(image, "rows", 2 * k)
        pieces += [piece, swap(piece, "rows", 1)]
    return back(me_rows, targets, kernels, pieces)


def solution(mesh):
    in_specs = (
        P("rows", None, "dist"),
        P("rows", None, None, None),
        P("rows", None),
        P("dist", "rows", None, None),
        P("dist"),
    )
    out_specs = P("rows", None, "dist")
    return jax.shard_map(shards, mesh=mesh, in_specs=in_specs, out_specs=out_specs, check_vma=False)
```

time: 403 us -> 68 us (0.17); the launches traced: 398 us -> 67.5 us
  blocking collectives: 232 us -> 0 us
  matrix products: 74.9 us -> 0 us
  other arithmetic: 44.7 us -> 0.75 us
  Pallas kernels: 0 us -> 21.7 us
  starting transfers between devices: 0.26 us -> 20.8 us
  between operations: 14.4 us -> 2.66 us
  local copies, waits for them, and re-layouts: 11.7 us -> 4.58 us
    all_to_all x1 -> x0, blocking collectives: 191 us -> none  [shards(): lax.all_to_all(outgoing, 'rows', split_axis=0, concat_axis=0, tiled=True)]
    dot_general x8 -> x0, matrix products: 74.9 us -> none  [the longest x2 40.1 us: synthesize(): lax.dot_general(coeffs * weight, table, (((1,), (1,)), ((), ())), precisi...]
    psum x1 -> x0, blocking collectives: 41 us -> none  [shards(): summed = lax.psum(term, 'dist')]
    cos x1 -> x0, other arithmetic: 34.4 us -> none  [spectral_table(): return jnp.concatenate([jnp.cos(turns), jnp.sin(turns)], axis=1)]
    pallas_call x0 -> x6, Pallas kernels: none -> 21.7 us  [the longest x1 5.59 us: project(): pl.pallas_call(project_kernel, out_shape=(out, out), grid_spec=pltpu.Pref...]
    ppermute x0 -> x20, starting transfers between devices: none -> 20.8 us  [swap(): return lax.ppermute(x, axis, [(i, i ^ mask) for i in range(size)])]
    all_gather x2 -> x0, waiting for transfers between devices: 20.7 us -> none  [the longest x1 20.7 us: shards(): piece = lax.all_gather(image_gradient[None], 'rows', axis=0, tiled=True)]
    ppermute x0 -> x20, waiting for transfers between devices: none -> 17 us  [swap(): return lax.ppermute(x, axis, [(i, i ^ mask) for i in range(size)])]
  transfers between devices with their start and end apart: 2 -> 20, of which waited for: 1 -> 9; matrix products, arithmetic and copies ran while one was open for 9% -> 1% of each run, Pallas kernels for 0% -> 9%
where the time goes in v1:
time: 68 us; the launch traced here: 67.5 us
  Pallas kernels  21.7 us (32%)
  starting transfers between devices  20.8 us (31%)
  waiting for transfers between devices  17 us (25%)
  local copies, waits for them, and re-layouts  4.58 us (7%)
  between operations  2.66 us (4%)
  other arithmetic  0.75 us (1%)
    ppermute x20, starting transfers between devices, swap(): return lax.ppermute(x, axis, [(i, i ^ mask) for i in range(size)])  20.8 us
    ppermute x20, waiting for transfers between devices, swap(): return lax.ppermute(x, axis, [(i, i ^ mask) for i in range(size)])  17 us
    pallas_call x1, Pallas kernels, project(): pl.pallas_call(project_kernel, out_shape=(out, out), grid_spec=pltpu.Pref...  5.59 us
    pallas_call x1, Pallas kernels, back(): pl.pallas_call(functools.partial(back_kernel, owners), out_shape=jax.Shap...  5.4 us
    unnamed x35, local copies, waits for them, and re-layouts  4.58 us
    pallas_call x1, Pallas kernels, tables(): pl.pallas_call(functools.partial(table_kernel, width), out_shape=[jax.Sha...  3.96 us
    pallas_call x1, Pallas kernels, filtered(): pl.pallas_call(functools.partial(filter_kernel, n_dist), out_shape=jax.Sh...  2.74 us
    pallas_call x1, Pallas kernels, pair_sum(): pl.pallas_call(pair_kernel, out_shape=[jax.ShapeDtypeStruct((blk, quarter...  2.09 us
  transfers between devices with their start and end apart: 20, of which 9 were waited for; matrix products, arithmetic and copies ran while one was open for 1% of the time, Pallas kernels for 9%

profile of v1, /device:TPU:0, one launch (start us, length us, event | category | flops | bytes accessed | tf_op | source)
XLA Modules:
  0.0 67.5 jit_solution(1556570343521409969)
XLA Ops:
  0.0 1.3 %copy.7.targets_ref = s32[16,2]{1,0:T(8,128)} copy(s32[16,2]{0,1:T(2,128)} %param.7) | data formatting | bytes 256 | tf_op args[2]
  1.3 5.6 %project.1 = (bf16[4,128,512]{2,1,0:T(8,128)(2,1)}, bf16[4,128,512]{2,1,0:T(8,128)(2,1)}) custom-call(s32[1]{0:T(128)} %bitcast.me_ref, s32[16,2]{1,0:T(8,128)} %copy.7.targets_ref, bf16[16,2,128,128]{3,2,1,0:T(8,128)(2,1)} %kernels_ref.3, bf16[16,128,512]{2,1,0:T(8,128)(2,1)} %volume_ref.1), custom_call_target="tpu_custom_call" | custom-call | flops 536870912 | bytes 4194304 | tf_op jit(solution)/shard_map/project/pallas_call | solution.py:62
  6.9 0.5 collective-permute-start
  7.4 2.5 %collective-permute-start.4 = (f32[1]{0:T(128)}, f32[1]{0:T(128)}, u32[]{:S(2)}, u32[]{:S(2)}) collective-permute-start(f32[1]{0:T(128)} %param.9), channel_id=1, source_target_pairs={{0,8},{8,0},{16,24},{24,16},{1,9},{9,1},{17,25},{25,17},{2,10},{10... | collective-permute-start | bytes 20 | tf_op jit(solution)/shard_map/ppermute | solution.py:22
  9.9 1.5 %collective-permute-start.6 = (f32[1]{0:T(128)}, f32[1]{0:T(128)}, u32[]{:S(2)}, u32[]{:S(2)}) collective-permute-start(f32[1]{0:T(128)} %param.9), channel_id=1, source_target_pairs={{0,24},{8,16},{16,8},{24,0},{1,25},{9,17},{17,9},{25,1},{2,26},{10... | collective-permute-start | bytes 20 | tf_op jit(solution)/shard_map/ppermute | solution.py:22
  11.4 0.0 collective-permute-start.5
  12.2 0.0 collective-permute-done.4
  12.8 1.9 %collective-permute-done.6 = f32[1]{0:T(128)} collective-permute-done((f32[1]{0:T(128)}, f32[1]{0:T(128)}, u32[]{:S(2)}, u32[]{:S(2)}) %collective-permute-start.6) | collective-permute-done | bytes 36 | tf_op jit(solution)/shard_map/ppermute | solution.py:22
  15.3 0.0 collective-permute-done.5
  15.9 0.1 fusion.10
  16.0 0.6 pad_maximum_fusion.spectra_ref
  16.6 0.0 collective-permute-done.came_ref
  16.6 0.8 %copy-done = bf16[4,128,512]{2,1,0:T(8,128)(2,1)} copy-done((bf16[4,128,512]{2,1,0:T(8,128)(2,1)}, bf16[4,128,512]{2,1,0:T(8,128)(2,1)S(1)}, u32[]{:S(2)}) %copy-start) | copy-done | bytes 524312
  17.4 2.1 %pair_sum.1 = (f32[128,512]{1,0:T(8,128)}, bf16[128,512]{1,0:T(8,128)(2,1)}, bf16[128,512]{1,0:T(8,128)(2,1)}, bf16[128,512]{1,0:T(8,128)(2,1)}) custom-call(bf16[4,128,512]{2,1,0:T(8,128)(2,1)} %get-tuple-element.18.keep_ref, bf16[4,128,512]{2,1,0:T(8,128)(2,1)} %copy-done), custom_call_target="tpu_custom_call" | custom-call | flops 262144 | bytes 1572864 | tf_op jit(solution)/shard_map/pair_sum/pallas_call | solution.py:91
  19.5 1.6 %collective-permute-start.1 = (bf16[128,512]{1,0:T(8,128)(2,1)}, bf16[128,512]{1,0:T(8,128)(2,1)S(1)}, u32[]{:S(2)}, u32[]{:S(2)}) collective-permute-start(bf16[128,512]{1,0:T(8,128)(2,1)} %get-tuple-element.21), channel_id=1, source_target_pairs={{0,2},{1,3},{2,0},{3,1},{4,6},{5,7},{6,4},{7,5},{8,10},{9,11},{10,... | collective-permute-start | bytes 393224 | tf_op jit(solution)/shard_map/ppermute | solution.py:22
  21.1 2.6 %collective-permute-start.2 = (bf16[128,512]{1,0:T(8,128)(2,1)}, bf16[128,512]{1,0:T(8,128)(2,1)S(1)}, u32[]{:S(2)}, u32[]{:S(2)}) collective-permute-start(bf16[128,512]{1,0:T(8,128)(2,1)} %get-tuple-element.22), channel_id=1, source_target_pairs={{0,4},{1,5},{2,6},{3,7},{4,0},{5,1},{6,2},{7,3},{8,12},{9,13},{10,... | collective-permute-start | bytes 393224 | tf_op jit(solution)/shard_map/ppermute | solution.py:22
  23.7 0.2 collective-permute-start.3
  23.9 4.0 %tables.1 = (bf16[256,2560]{1,0:T(8,128)(2,1)}, bf16[128,512]{1,0:T(8,128)(2,1)}, bf16[128,512]{1,0:T(8,128)(2,1)}, bf16[128,512]{1,0:T(8,128)(2,1)}, bf16[128,512]{1,0:T(8,128)(2,1)}) custom-call(f32[32,128]{1,0:T(8,128)} %pad_maximum_fusion.spectra_ref, bf16[128,2048]{1,0:T(8,128)(2,1)} %bitcast.7, s32[1]{0:T(128)} %bitcast.1.me_ref), custom_call_target="tpu_custom_call" | custom-call | flops 1073741824 | bytes 3145728 | tf_op jit(solution)/shard_map/tables/pallas_call | solution.py:193
  27.9 1.3 %collective-permute-start.10 = (bf16[128,512]{1,0:T(8,128)(2,1)}, bf16[128,512]{1,0:T(8,128)(2,1)S(1)}, u32[]{:S(2)}, u32[]{:S(2)}) collective-permute-start(bf16[128,512]{1,0:T(8,128)(2,1)} %get-tuple-element.28), channel_id=1, source_target_pairs={{0,8},{8,0},{16,24},{24,16},{1,9},{9,1},{17,25},{25,17},{2,10},{10... | collective-permute-start | bytes 393224 | tf_op jit(solution)/shard_map/ppermute | solution.py:22
  29.2 0.8 %collective-permute-start.11 = (bf16[128,512]{1,0:T(8,128)(2,1)}, bf16[128,512]{1,0:T(8,128)(2,1)S(1)}, u32[]{:S(2)}, u32[]{:S(2)}) collective-permute-start(bf16[128,512]{1,0:T(8,128)(2,1)} %get-tuple-element.29), channel_id=1, source_target_pairs={{0,16},{8,24},{16,0},{24,8},{1,17},{9,25},{17,1},{25,9},{2,18},{10... | collective-permute-start | bytes 393224 | tf_op jit(solution)/shard_map/ppermute | solution.py:22
  29.9 0.0 collective-permute-done.1.refs_0_
  29.9 1.4 %collective-permute-start.12 = (bf16[128,512]{1,0:T(8,128)(2,1)}, bf16[128,512]{1,0:T(8,128)(2,1)S(1)}, u32[]{:S(2)}, u32[]{:S(2)}) collective-permute-start(bf16[128,512]{1,0:T(8,128)(2,1)} %get-tuple-element.30), channel_id=1, source_target_pairs={{0,24},{8,16},{16,8},{24,0},{1,25},{9,17},{17,9},{25,1},{2,26},{10... | collective-permute-start | bytes 393224 | tf_op jit(solution)/shard_map/ppermute | solution.py:22
  31.4 2.0 %collective-permute-done.2.refs_1_ = bf16[128,512]{1,0:T(8,128)(2,1)S(1)} collective-permute-done((bf16[128,512]{1,0:T(8,128)(2,1)}, bf16[128,512]{1,0:T(8,128)(2,1)S(1)}, u32[]{:S(2)}, u32[]{:S(2)}) %collective-permute-start.2) | collective-permute-done | bytes 131104 | tf_op jit(solution)/shard_map/ppermute | solution.py:22
  33.3 0.0 collective-permute-done.3.refs_2_
  33.3 0.0 copy-done.6
  33.3 0.6 copy-done.8
  34.0 0.1 copy-done.11
  34.0 1.9 %total_sum.1 = (f32[128,512]{1,0:T(8,128)}, bf16[128,512]{1,0:T(8,128)(2,1)}) custom-call(f32[128,512]{1,0:T(8,128)} %get-tuple-element.20.own_ref, bf16[128,512]{1,0:T(8,128)(2,1)} %copy-done.6, bf16[128,512]{1,0:T(8,128)(2,1)} %copy-done.8, bf16[128,512]{1,0:T(8,128)(2,1)} %copy-done.11), custom_call_target="tpu_custom_call" | custom-call | flops 196608 | bytes 524288 | tf_op jit(solution)/shard_map/total_sum/pallas_call | solution.py:112
  35.9 1.8 %collective-permute-start.9 = (bf16[128,512]{1,0:T(8,128)(2,1)}, bf16[128,512]{1,0:T(8,128)(2,1)S(1)}, u32[]{:S(2)}, u32[]{:S(2)}) collective-permute-start(bf16[128,512]{1,0:T(8,128)(2,1)} %get-tuple-element.26.refs_0_), channel_id=1, source_target_pairs={{0,24},{8,16},{16,8},{24,0},{1,25},{9,17},{17,9},{25,1},{2,26},{10... | collective-permute-start | bytes 393224 | tf_op jit(solution)/shard_map/ppermute | solution.py:22
  37.7 1.0 %collective-permute-start.8 = (bf16[128,512]{1,0:T(8,128)(2,1)}, bf16[128,512]{1,0:T(8,128)(2,1)S(1)}, u32[]{:S(2)}, u32[]{:S(2)}) collective-permute-start(bf16[128,512]{1,0:T(8,128)(2,1)} %get-tuple-element.26.refs_0_), channel_id=1, source_target_pairs={{0,16},{8,24},{16,0},{24,8},{1,17},{9,25},{17,1},{25,9},{2,18},{10... | collective-permute-start | bytes 393224 | tf_op jit(solution)/shard_map/ppermute | solution.py:22
  38.7 0.0 collective-permute-done.10.refs_5_
  38.7 0.7 %collective-permute-start.7 = (bf16[128,512]{1,0:T(8,128)(2,1)}, bf16[128,512]{1,0:T(8,128)(2,1)S(1)}, u32[]{:S(2)}, u32[]{:S(2)}) collective-permute-start(bf16[128,512]{1,0:T(8,128)(2,1)} %get-tuple-element.26.refs_0_), channel_id=1, source_target_pairs={{0,8},{8,0},{16,24},{24,16},{1,9},{9,1},{17,25},{25,17},{2,10},{10... | collective-permute-start | bytes 393224 | tf_op jit(solution)/shard_map/ppermute | solution.py:22
  39.4 0.0 collective-permute-done.11.refs_6_
  39.4 0.0 collective-permute-done.12.refs_7_
  39.4 0.0 copy-start.3
  39.5 2.6 %collective-permute-done.9.refs_3_ = bf16[128,512]{1,0:T(8,128)(2,1)S(1)} collective-permute-done((bf16[128,512]{1,0:T(8,128)(2,1)}, bf16[128,512]{1,0:T(8,128)(2,1)S(1)}, u32[]{:S(2)}, u32[]{:S(2)}) %collective-permute-start.9) | collective-permute-done | bytes 131104 | tf_op jit(solution)/shard_map/ppermute | solution.py:22
  42.1 1.3 %collective-permute-done.8.refs_2_ = bf16[128,512]{1,0:T(8,128)(2,1)S(1)} collective-permute-done((bf16[128,512]{1,0:T(8,128)(2,1)}, bf16[128,512]{1,0:T(8,128)(2,1)S(1)}, u32[]{:S(2)}, u32[]{:S(2)}) %collective-permute-start.8) | collective-permute-done | bytes 131104 | tf_op jit(solution)/shard_map/ppermute | solution.py:22
  43.4 0.5 collective-permute-done.7.refs_1_
  43.9 0.0 copy-done.1
  43.9 0.0 copy-done.2
  43.9 0.0 copy-done.3
  43.9 0.0 copy-done.9
  43.9 0.2 copy-done.12
  44.1 0.5 copy-done.14
  44.6 2.7 %filter.1.refs_0_ = bf16[128,512]{1,0:T(8,128)(2,1)} custom-call(s32[1]{0:T(128)} %bitcast.1.me_ref, f32[128,512]{1,0:T(8,128)} %get-tuple-element.24.own_ref, bf16[256,2560]{1,0:T(8,128)(2,1)} %get-tuple-element.25.table_ref, bf16[128,512]{1,0:T(8,128)(2,1)} %get-tuple-element.26.refs_0_, bf16[128,512]{1,0:T(8,128)(2,1)} %copy-done.14, ...), custom_call_target="tpu_custom_call" | custom-call | flops 268435456 | bytes 3145728 | tf_op jit(solution)/shard_map/filter/pallas_call | solution.py:228
  47.3 2.5 %collective-permute-start.18 = (bf16[128,512]{1,0:T(8,128)(2,1)}, bf16[128,512]{1,0:T(8,128)(2,1)S(1)}, u32[]{:S(2)}, u32[]{:S(2)}) collective-permute-start(bf16[128,512]{1,0:T(8,128)(2,1)} %filter.1.refs_0_), channel_id=1, source_target_pairs={{0,6},{1,7},{2,4},{3,5},{4,2},{5,3},{6,0},{7,1},{8,14},{9,15},{10,... | collective-permute-start | bytes 393224 | tf_op jit(solution)/shard_map/ppermute | solution.py:22
  49.8 1.0 %collective-permute-start.16 = (bf16[128,512]{1,0:T(8,128)(2,1)}, bf16[128,512]{1,0:T(8,128)(2,1)S(1)}, u32[]{:S(2)}, u32[]{:S(2)}) collective-permute-start(bf16[128,512]{1,0:T(8,128)(2,1)} %filter.1.refs_0_), channel_id=1, source_target_pairs={{0,4},{1,5},{2,6},{3,7},{4,0},{5,1},{6,2},{7,3},{8,12},{9,13},{10,... | collective-permute-start | bytes 393224 | tf_op jit(solution)/shard_map/ppermute | solution.py:22
  50.8 0.9 %collective-permute-start.14 = (bf16[128,512]{1,0:T(8,128)(2,1)}, bf16[128,512]{1,0:T(8,128)(2,1)S(1)}, u32[]{:S(2)}, u32[]{:S(2)}) collective-permute-start(bf16[128,512]{1,0:T(8,128)(2,1)} %filter.1.refs_0_), channel_id=1, source_target_pairs={{0,2},{1,3},{2,0},{3,1},{4,6},{5,7},{6,4},{7,5},{8,10},{9,11},{10,... | collective-permute-start | bytes 393224 | tf_op jit(solution)/shard_map/ppermute | solution.py:22
  51.7 0.0 collective-permute-start.13
  51.7 3.8 %collective-permute-done.18.refs_6_ = bf16[128,512]{1,0:T(8,128)(2,1)S(1)} collective-permute-done((bf16[128,512]{1,0:T(8,128)(2,1)}, bf16[128,512]{1,0:T(8,128)(2,1)S(1)}, u32[]{:S(2)}, u32[]{:S(2)}) %collective-permute-start.18) | collective-permute-done | bytes 131104 | tf_op jit(solution)/shard_map/ppermute | solution.py:22
  55.5 0.0 collective-permute-start.19
  55.5 4.0 %collective-permute-done.16.refs_4_ = bf16[128,512]{1,0:T(8,128)(2,1)S(1)} collective-permute-done((bf16[128,512]{1,0:T(8,128)(2,1)}, bf16[128,512]{1,0:T(8,128)(2,1)S(1)}, u32[]{:S(2)}, u32[]{:S(2)}) %collective-permute-start.16) | collective-permute-done | bytes 131104 | tf_op jit(solution)/shard_map/ppermute | solution.py:22
  59.5 0.0 collective-permute-start.17
  59.5 0.0 collective-permute-done.14.refs_2_
  59.5 0.5 collective-permute-start.15
  60.0 0.0 collective-permute-done.13.refs_1_
  60.0 0.0 collective-permute-done.19.refs_7_
  60.0 0.8 %collective-permute-done.17.refs_5_ = bf16[128,512]{1,0:T(8,128)(2,1)S(1)} collective-permute-done((bf16[128,512]{1,0:T(8,128)(2,1)S(1)}, bf16[128,512]{1,0:T(8,128)(2,1)S(1)}, u32[]{:S(2)}, u32[]{:S(2)}) %collective-permute-start.17) | collective-permute-done | bytes 131104 | tf_op jit(solution)/shard_map/ppermute | solution.py:22
  60.8 0.2 collective-permute-done.15.refs_3_
  61.0 0.0 copy-done.10
  61.0 0.0 copy-done.13
  61.0 0.4 copy-done.15
  61.5 0.6 copy-done.16
  62.1 5.4 %back.1 = bf16[16,128,512]{2,1,0:T(8,128)(2,1)} custom-call(s32[1]{0:T(128)} %bitcast.me_ref, s32[16,2]{1,0:T(8,128)} %copy.7.targets_ref, bf16[16,2,128,128]{3,2,1,0:T(8,128)(2,1)} %kernels_ref.3, bf16[128,512]{1,0:T(8,128)(2,1)} %filter.1.refs_0_, bf16[128,512]{1,0:T(8,128)(2,1)} %copy-done.10, bf16[128,512]{1,0:T(8,128)(2,1)} %copy-done.7, ...), custom_call_target="tpu_custom_call" | custom-call | flops 536870912 | bytes 4194304 | tf_op jit(solution)/shard_map/back/pallas_call | solution.py:265
  (20 shorter events, 0.0 us)
Async XLA Ops:
  6.9 9.7 %collective-permute-start = (bf16[4,128,512]{2,1,0:T(8,128)(2,1)}, bf16[4,128,512]{2,1,0:T(8,128)(2,1)S(1)}, u32[]{:S(2)}, u32[]{:S(2)}) collective-permute-start(bf16[4,128,512]{2,1,0:T(8,128)(2,1)} %get-tuple-element.19), channel_id=1, source_target_pairs={{0,1},{1,0},{2,3},{3,2},{4,5},{5,4},{6,7},{7,6},{8,9},{9,8},{10,11... | collective-permute-start | bytes 1572872 | tf_op jit(solution)/shard_map/ppermute | solution.py:22
  7.4 4.8 %collective-permute-start.4 = (f32[1]{0:T(128)}, f32[1]{0:T(128)}, u32[]{:S(2)}, u32[]{:S(2)}) collective-permute-start(f32[1]{0:T(128)} %param.9), channel_id=1, source_target_pairs={{0,8},{8,0},{16,24},{24,16},{1,9},{9,1},{17,25},{25,17},{2,10},{10... | collective-permute-start | bytes 20 | tf_op jit(solution)/shard_map/ppermute | solution.py:22
  9.9 4.7 %collective-permute-start.6 = (f32[1]{0:T(128)}, f32[1]{0:T(128)}, u32[]{:S(2)}, u32[]{:S(2)}) collective-permute-start(f32[1]{0:T(128)} %param.9), channel_id=1, source_target_pairs={{0,24},{8,16},{16,8},{24,0},{1,25},{9,17},{17,9},{25,1},{2,26},{10... | collective-permute-start | bytes 20 | tf_op jit(solution)/shard_map/ppermute | solution.py:22
  11.4 3.9 %collective-permute-start.5 = (f32[1]{0:T(128)}, f32[1]{0:T(128)}, u32[]{:S(2)}, u32[]{:S(2)}) collective-permute-start(f32[1]{0:T(128)} %param.9), channel_id=1, source_target_pairs={{0,16},{8,24},{16,0},{24,8},{1,17},{9,25},{17,1},{25,9},{2,18},{10... | collective-permute-start | bytes 20 | tf_op jit(solution)/shard_map/ppermute | solution.py:22
  16.6 0.8 %copy-start = (bf16[4,128,512]{2,1,0:T(8,128)(2,1)}, bf16[4,128,512]{2,1,0:T(8,128)(2,1)S(1)}, u32[]{:S(2)}) copy-start(bf16[4,128,512]{2,1,0:T(8,128)(2,1)S(1)} %collective-permute-done.came_ref) | copy-start | bytes 1572868
  19.5 10.4 %collective-permute-start.1 = (bf16[128,512]{1,0:T(8,128)(2,1)}, bf16[128,512]{1,0:T(8,128)(2,1)S(1)}, u32[]{:S(2)}, u32[]{:S(2)}) collective-permute-start(bf16[128,512]{1,0:T(8,128)(2,1)} %get-tuple-element.21), channel_id=1, source_target_pairs={{0,2},{1,3},{2,0},{3,1},{4,6},{5,7},{6,4},{7,5},{8,10},{9,11},{10,... | collective-permute-start | bytes 393224 | tf_op jit(solution)/shard_map/ppermute | solution.py:22
  21.1 12.2 %collective-permute-start.2 = (bf16[128,512]{1,0:T(8,128)(2,1)}, bf16[128,512]{1,0:T(8,128)(2,1)S(1)}, u32[]{:S(2)}, u32[]{:S(2)}) collective-permute-start(bf16[128,512]{1,0:T(8,128)(2,1)} %get-tuple-element.22), channel_id=1, source_target_pairs={{0,4},{1,5},{2,6},{3,7},{4,0},{5,1},{6,2},{7,3},{8,12},{9,13},{10,... | collective-permute-start | bytes 393224 | tf_op jit(solution)/shard_map/ppermute | solution.py:22
  23.7 9.6 %collective-permute-start.3 = (bf16[128,512]{1,0:T(8,128)(2,1)}, bf16[128,512]{1,0:T(8,128)(2,1)S(1)}, u32[]{:S(2)}, u32[]{:S(2)}) collective-permute-start(bf16[128,512]{1,0:T(8,128)(2,1)} %get-tuple-element.23), channel_id=1, source_target_pairs={{0,6},{1,7},{2,4},{3,5},{4,2},{5,3},{6,0},{7,1},{8,14},{9,15},{10,... | collective-permute-start | bytes 393224 | tf_op jit(solution)/shard_map/ppermute | solution.py:22
  27.9 10.9 %collective-permute-start.10 = (bf16[128,512]{1,0:T(8,128)(2,1)}, bf16[128,512]{1,0:T(8,128)(2,1)S(1)}, u32[]{:S(2)}, u32[]{:S(2)}) collective-permute-start(bf16[128,512]{1,0:T(8,128)(2,1)} %get-tuple-element.28), channel_id=1, source_target_pairs={{0,8},{8,0},{16,24},{24,16},{1,9},{9,1},{17,25},{25,17},{2,10},{10... | collective-permute-start | bytes 393224 | tf_op jit(solution)/shard_map/ppermute | solution.py:22
  29.2 10.3 %collective-permute-start.11 = (bf16[128,512]{1,0:T(8,128)(2,1)}, bf16[128,512]{1,0:T(8,128)(2,1)S(1)}, u32[]{:S(2)}, u32[]{:S(2)}) collective-permute-start(bf16[128,512]{1,0:T(8,128)(2,1)} %get-tuple-element.29), channel_id=1, source_target_pairs={{0,16},{8,24},{16,0},{24,8},{1,17},{9,25},{17,1},{25,9},{2,18},{10... | collective-permute-start | bytes 393224 | tf_op jit(solution)/shard_map/ppermute | solution.py:22
  29.9 3.4 %copy-start.6 = (bf16[128,512]{1,0:T(8,128)(2,1)}, bf16[128,512]{1,0:T(8,128)(2,1)S(1)}, u32[]{:S(2)}) copy-start(bf16[128,512]{1,0:T(8,128)(2,1)S(1)} %collective-permute-done.1.refs_0_) | copy-start | bytes 393220
  29.9 9.5 %collective-permute-start.12 = (bf16[128,512]{1,0:T(8,128)(2,1)}, bf16[128,512]{1,0:T(8,128)(2,1)S(1)}, u32[]{:S(2)}, u32[]{:S(2)}) collective-permute-start(bf16[128,512]{1,0:T(8,128)(2,1)} %get-tuple-element.30), channel_id=1, source_target_pairs={{0,24},{8,16},{16,8},{24,0},{1,25},{9,17},{17,9},{25,1},{2,26},{10... | collective-permute-start | bytes 393224 | tf_op jit(solution)/shard_map/ppermute | solution.py:22
  33.3 0.6 copy-start.8
  33.3 0.7 %copy-start.11 = (bf16[128,512]{1,0:T(8,128)(2,1)}, bf16[128,512]{1,0:T(8,128)(2,1)S(1)}, u32[]{:S(2)}) copy-start(bf16[128,512]{1,0:T(8,128)(2,1)S(1)} %collective-permute-done.3.refs_2_) | copy-start | bytes 393220
  35.9 6.1 %collective-permute-start.9 = (bf16[128,512]{1,0:T(8,128)(2,1)}, bf16[128,512]{1,0:T(8,128)(2,1)S(1)}, u32[]{:S(2)}, u32[]{:S(2)}) collective-permute-start(bf16[128,512]{1,0:T(8,128)(2,1)} %get-tuple-element.26.refs_0_), channel_id=1, source_target_pairs={{0,24},{8,16},{16,8},{24,0},{1,25},{9,17},{17,9},{25,1},{2,26},{10... | collective-permute-start | bytes 393224 | tf_op jit(solution)/shard_map/ppermute | solution.py:22
  37.7 5.7 %collective-permute-start.8 = (bf16[128,512]{1,0:T(8,128)(2,1)}, bf16[128,512]{1,0:T(8,128)(2,1)S(1)}, u32[]{:S(2)}, u32[]{:S(2)}) collective-permute-start(bf16[128,512]{1,0:T(8,128)(2,1)} %get-tuple-element.26.refs_0_), channel_id=1, source_target_pairs={{0,16},{8,24},{16,0},{24,8},{1,17},{9,25},{17,1},{25,9},{2,18},{10... | collective-permute-start | bytes 393224 | tf_op jit(solution)/shard_map/ppermute | solution.py:22
  38.7 5.2 %copy-start.1 = (bf16[128,512]{1,0:T(8,128)(2,1)}, bf16[128,512]{1,0:T(8,128)(2,1)S(1)}, u32[]{:S(2)}) copy-start(bf16[128,512]{1,0:T(8,128)(2,1)S(1)} %collective-permute-done.10.refs_5_) | copy-start | bytes 393220
  38.7 5.2 %collective-permute-start.7 = (bf16[128,512]{1,0:T(8,128)(2,1)}, bf16[128,512]{1,0:T(8,128)(2,1)S(1)}, u32[]{:S(2)}, u32[]{:S(2)}) collective-permute-start(bf16[128,512]{1,0:T(8,128)(2,1)} %get-tuple-element.26.refs_0_), channel_id=1, source_target_pairs={{0,8},{8,0},{16,24},{24,16},{1,9},{9,1},{17,25},{25,17},{2,10},{10... | collective-permute-start | bytes 393224 | tf_op jit(solution)/shard_map/ppermute | solution.py:22
  39.4 4.5 %copy-start.2 = (bf16[128,512]{1,0:T(8,128)(2,1)}, bf16[128,512]{1,0:T(8,128)(2,1)S(1)}, u32[]{:S(2)}) copy-start(bf16[128,512]{1,0:T(8,128)(2,1)S(1)} %collective-permute-done.11.refs_6_) | copy-start | bytes 393220
  39.4 4.5 %copy-start.3 = (bf16[128,512]{1,0:T(8,128)(2,1)}, bf16[128,512]{1,0:T(8,128)(2,1)S(1)}, u32[]{:S(2)}) copy-start(bf16[128,512]{1,0:T(8,128)(2,1)S(1)} %collective-permute-done.12.refs_7_) | copy-start | bytes 393220
  42.1 1.8 %copy-start.9 = (bf16[128,512]{1,0:T(8,128)(2,1)}, bf16[128,512]{1,0:T(8,128)(2,1)S(1)}, u32[]{:S(2)}) copy-start(bf16[128,512]{1,0:T(8,128)(2,1)S(1)} %collective-permute-done.9.refs_3_) | copy-start | bytes 393220
  43.4 0.7 copy-start.12
  43.9 0.7 copy-start.14
  47.3 8.2 %collective-permute-start.18 = (bf16[128,512]{1,0:T(8,128)(2,1)}, bf16[128,512]{1,0:T(8,128)(2,1)S(1)}, u32[]{:S(2)}, u32[]{:S(2)}) collective-permute-start(bf16[128,512]{1,0:T(8,128)(2,1)} %filter.1.refs_0_), channel_id=1, source_target_pairs={{0,6},{1,7},{2,4},{3,5},{4,2},{5,3},{6,0},{7,1},{8,14},{9,15},{10,... | collective-permute-start | bytes 393224 | tf_op jit(solution)/shard_map/ppermute | solution.py:22
  49.8 9.7 %collective-permute-start.16 = (bf16[128,512]{1,0:T(8,128)(2,1)}, bf16[128,512]{1,0:T(8,128)(2,1)S(1)}, u32[]{:S(2)}, u32[]{:S(2)}) collective-permute-start(bf16[128,512]{1,0:T(8,128)(2,1)} %filter.1.refs_0_), channel_id=1, source_target_pairs={{0,4},{1,5},{2,6},{3,7},{4,0},{5,1},{6,2},{7,3},{8,12},{9,13},{10,... | collective-permute-start | bytes 393224 | tf_op jit(solution)/shard_map/ppermute | solution.py:22
  50.8 8.7 %collective-permute-start.14 = (bf16[128,512]{1,0:T(8,128)(2,1)}, bf16[128,512]{1,0:T(8,128)(2,1)S(1)}, u32[]{:S(2)}, u32[]{:S(2)}) collective-permute-start(bf16[128,512]{1,0:T(8,128)(2,1)} %filter.1.refs_0_), channel_id=1, source_target_pairs={{0,2},{1,3},{2,0},{3,1},{4,6},{5,7},{6,4},{7,5},{8,10},{9,11},{10,... | collective-permute-start | bytes 393224 | tf_op jit(solution)/shard_map/ppermute | solution.py:22
  51.7 8.3 %collective-permute-start.13 = (bf16[128,512]{1,0:T(8,128)(2,1)}, bf16[128,512]{1,0:T(8,128)(2,1)S(1)}, u32[]{:S(2)}, u32[]{:S(2)}) collective-permute-start(bf16[128,512]{1,0:T(8,128)(2,1)} %filter.1.refs_0_), channel_id=1, source_target_pairs={{0,1},{1,0},{2,3},{3,2},{4,5},{5,4},{6,7},{7,6},{8,9},{9,8},{10,11... | collective-permute-start | bytes 393224 | tf_op jit(solution)/shard_map/ppermute | solution.py:22
  55.5 5.5 %copy-start.4 = (bf16[128,512]{1,0:T(8,128)(2,1)}, bf16[128,512]{1,0:T(8,128)(2,1)S(1)}, u32[]{:S(2)}) copy-start(bf16[128,512]{1,0:T(8,128)(2,1)S(1)} %collective-permute-done.18.refs_6_) | copy-start | bytes 393220
  55.5 4.5 %collective-permute-start.19 = (bf16[128,512]{1,0:T(8,128)(2,1)S(1)}, bf16[128,512]{1,0:T(8,128)(2,1)S(1)}, u32[]{:S(2)}, u32[]{:S(2)}) collective-permute-start(bf16[128,512]{1,0:T(8,128)(2,1)S(1)} %collective-permute-done.18.refs_6_), channel_id=1, source_target_pairs={{0,1},{1,0},{2,3},{3,2},{4,5},{5,4},{6,7},{7,6},{8,9},{9,8},{10,11... | collective-permute-start | bytes 393224 | tf_op jit(solution)/shard_map/ppermute | solution.py:22
  59.5 1.5 %copy-start.5 = (bf16[128,512]{1,0:T(8,128)(2,1)}, bf16[128,512]{1,0:T(8,128)(2,1)S(1)}, u32[]{:S(2)}) copy-start(bf16[128,512]{1,0:T(8,128)(2,1)S(1)} %collective-permute-done.16.refs_4_) | copy-start | bytes 393220
  59.5 1.3 %collective-permute-start.17 = (bf16[128,512]{1,0:T(8,128)(2,1)S(1)}, bf16[128,512]{1,0:T(8,128)(2,1)S(1)}, u32[]{:S(2)}, u32[]{:S(2)}) collective-permute-start(bf16[128,512]{1,0:T(8,128)(2,1)S(1)} %collective-permute-done.16.refs_4_), channel_id=1, source_target_pairs={{0,1},{1,0},{2,3},{3,2},{4,5},{5,4},{6,7},{7,6},{8,9},{9,8},{10,11... | collective-permute-start | bytes 393224 | tf_op jit(solution)/shard_map/ppermute | solution.py:22
  59.5 1.5 %copy-start.7 = (bf16[128,512]{1,0:T(8,128)(2,1)}, bf16[128,512]{1,0:T(8,128)(2,1)S(1)}, u32[]{:S(2)}) copy-start(bf16[128,512]{1,0:T(8,128)(2,1)S(1)} %collective-permute-done.14.refs_2_) | copy-start | bytes 393220
  59.5 1.5 %collective-permute-start.15 = (bf16[128,512]{1,0:T(8,128)(2,1)S(1)}, bf16[128,512]{1,0:T(8,128)(2,1)S(1)}, u32[]{:S(2)}, u32[]{:S(2)}) collective-permute-start(bf16[128,512]{1,0:T(8,128)(2,1)S(1)} %collective-permute-done.14.refs_2_), channel_id=1, source_target_pairs={{0,1},{1,0},{2,3},{3,2},{4,5},{5,4},{6,7},{7,6},{8,9},{9,8},{10,11... | collective-permute-start | bytes 393224 | tf_op jit(solution)/shard_map/ppermute | solution.py:22
  60.0 1.0 %copy-start.10 = (bf16[128,512]{1,0:T(8,128)(2,1)}, bf16[128,512]{1,0:T(8,128)(2,1)S(1)}, u32[]{:S(2)}) copy-start(bf16[128,512]{1,0:T(8,128)(2,1)S(1)} %collective-permute-done.13.refs_1_) | copy-start | bytes 393220
  60.0 1.0 %copy-start.13 = (bf16[128,512]{1,0:T(8,128)(2,1)}, bf16[128,512]{1,0:T(8,128)(2,1)S(1)}, u32[]{:S(2)}) copy-start(bf16[128,512]{1,0:T(8,128)(2,1)S(1)} %collective-permute-done.19.refs_7_) | copy-start | bytes 393220
  60.8 0.7 copy-start.15
  61.5 0.7 copy-start.16

commit v2 on v0

v2 whole, which is shorter than its diff:
```python
import functools
import math

import jax
import jax.numpy as jnp
from jax import lax
from jax.experimental import pallas as pl
from jax.experimental.pallas import tpu as pltpu
from jax.sharding import PartitionSpec as P


BF16 = jnp.bfloat16
F32 = jnp.float32
DEEP = 256
SPLIT = (1, 1)
MIB = 2**20


def whole(memory_space=pltpu.VMEM):
    return pl.BlockSpec(memory_space=memory_space)


def swap(x, axis, mask):
    size = lax.axis_size(axis)
    return lax.ppermute(x, axis, [(i, i ^ mask) for i in range(size)])


def chunks_of(blk):
    unit = blk // sum(SPLIT)
    starts = [unit * sum(SPLIT[:i]) for i in range(len(SPLIT))]
    return [(start, unit * size) for start, size in zip(starts, SPLIT)]


def cost(flops, nbytes):
    return pl.CostEstimate(flops=flops, bytes_accessed=nbytes, transcendentals=0)


def room(nbytes):
    return pltpu.CompilerParams(vmem_limit_bytes=int(nbytes) + 4 * MIB)


def project_kernel(me_ref, *refs):
    targets_hbm, kernels_hbm, volume_hbm, send_ref, keep_ref = refs[:5]
    targets, kernels, volume, acc, sems, target_sem = refs[5:]
    vblocks, top, blk, _ = kernels.shape
    half = send_ref.shape[0]

    group = 4
    steps = vblocks // group

    def copies(step):
        part = pl.ds(step * group, group)
        return (
            pltpu.make_async_copy(volume_hbm.at[part], volume.at[part], sems.at[0, step]),
            pltpu.make_async_copy(kernels_hbm.at[part], kernels.at[part], sems.at[1, step]),
        )

    get_targets = pltpu.make_async_copy(targets_hbm, targets, target_sem)
    get_targets.start()
    for step in range(steps):
        for copy in copies(step):
            copy.start()
    acc[...] = jnp.zeros_like(acc)
    get_targets.wait()
    me = me_ref[0]

    def body(step, carry):
        for copy in copies(step):
            copy.wait()
        for i in range(group):
            b = step * group + i
            product = jnp.dot(
                kernels[b].reshape(top * blk, blk), volume[b], preferred_element_type=F32
            )
            for t in range(top):
                rel = targets[t, b] ^ me
                slot = (rel & 1) * half + (rel >> 1)
                acc[slot] += product[t * blk : (t + 1) * blk]
        return carry

    lax.fori_loop(0, steps, body, 0)
    send_ref[...] = acc[half:].astype(BF16)
    keep_ref[...] = acc[:half].astype(BF16)


def project(me, targets, kernels, volume, owners):
    vblocks, blk, quarter = volume.shape
    top = kernels.shape[1]
    half = owners // 2
    out = jax.ShapeDtypeStruct((half, blk, quarter), BF16)
    return pl.pallas_call(
        project_kernel,
        out_shape=(out, out),
        in_specs=[whole(pltpu.SMEM)] + [whole(pltpu.HBM)] * 3,
        out_specs=[whole()] * 2,
        scratch_shapes=[
            pltpu.SMEM(targets.shape, jnp.int32),
            pltpu.VMEM(kernels.shape, BF16),
            pltpu.VMEM(volume.shape, BF16),
            pltpu.VMEM((owners, blk, quarter), F32),
            pltpu.SemaphoreType.DMA((2, vblocks)),
            pltpu.SemaphoreType.DMA,
        ],
        compiler_params=room(8 * owners * blk * quarter + 8 * MIB),
        cost_estimate=cost(2 * vblocks * top * blk * blk * quarter, 4 * MIB),
        name="project",
    )(me, *(pltpu.with_memory_space_constraint(x, pltpu.HBM) for x in (targets, kernels, volume)))


def pair_kernel(chunks, keep_ref, came_ref, *out_refs):
    half, blk, _ = keep_ref.shape
    rows = blk // chunks
    for i, ref in enumerate(out_refs):
        c, k = divmod(i, half)
        part = slice(c * rows, (c + 1) * rows)
        total = keep_ref[k, part].astype(F32) + came_ref[k, part].astype(F32)
        ref[...] = total.astype(ref.dtype)


def pair_sum(keep, came, chunks):
    half, blk, quarter = keep.shape
    rows = blk // chunks
    outs = [jax.ShapeDtypeStruct((rows, quarter), BF16 if k else F32) for k in range(half)]
    return pl.pallas_call(
        functools.partial(pair_kernel, chunks),
        out_shape=outs * chunks,
        in_specs=[whole()] * 2,
        out_specs=[whole()] * (half * chunks),
        compiler_params=room(8 * half * blk * quarter),
        cost_estimate=cost(half * blk * quarter, 6 * half * blk * quarter),
        name="pair_sum",
    )(keep, came)


def total_kernel(own_ref, *refs):
    n = len(SPLIT)
    came, total_refs, rounded_refs = refs[: -2 * n], refs[-2 * n : -n], refs[-n:]
    for c, (start, rows) in enumerate(chunks_of(own_ref.shape[0])):
        part = slice(start, start + rows)
        total = own_ref[part]
        for ref in came:
            total += ref[part].astype(F32)
        total_refs[c][...] = total
        rounded_refs[c][...] = total.astype(BF16)


def total_sum(own, came):
    blk, quarter = own.shape
    shapes = [(rows, quarter) for _, rows in chunks_of(blk)]
    outs = pl.pallas_call(
        total_kernel,
        out_shape=[jax.ShapeDtypeStruct(shape, d) for d in (F32, BF16) for shape in shapes],
        in_specs=[whole()] * (1 + len(came)),
        out_specs=[whole()] * (2 * len(shapes)),
        compiler_params=room((10 + 2 * len(came)) * own.size),
        cost_estimate=cost(own.size * len(came), 8 * own.size),
        name="total_sum",
    )(own, *came)
    return outs[: len(shapes)], outs[len(shapes) :]


def mm(a, b):
    return jnp.dot(a, b, precision=lax.Precision.HIGHEST, preferred_element_type=F32)


def turns(shape, period):
    a = lax.broadcasted_iota(jnp.int32, shape, 0)
    b = lax.broadcasted_iota(jnp.int32, shape, 1)
    angle = (a * b % period).astype(F32) * (2.0 * math.pi / period)
    return jnp.cos(angle), jnp.sin(angle)


def frequencies(short, long):
    k1 = lax.broadcasted_iota(jnp.int32, (short, long), 0)
    k2 = lax.broadcasted_iota(jnp.int32, (short, long), 1)
    freq = k1 + short * k2
    return jnp.minimum(freq, short * long - freq).astype(F32)


def circulant(spec):
    short, long = spec.shape
    width = short * long
    long_c, long_s = turns((long, long), long)
    twist_c, twist_s = turns((short, long), width)
    short_c, short_s = turns((short, short), short)
    yc, ys = mm(spec, long_c), mm(spec, long_s)
    re = yc * twist_c - ys * twist_s
    im = yc * twist_s + ys * twist_c
    g = (mm(short_c, re) - mm(short_s, im)) * (1.0 / width)
    line = jnp.concatenate([g[i : i + 1] for i in range(short)], axis=1)
    spread = jnp.broadcast_to(line, (DEEP, width))
    return pltpu.roll(spread, 0, 1, stride=1, stride_axis=0).astype(BF16)


def circ_kernel(number_ref, table_ref):
    width = table_ref.shape[1] // 2
    short, long = width // 128, 128
    freq = frequencies(short, long)
    number = jnp.full((short, long), number_ref[0], F32)
    matrix = circulant(2.0 * jnp.sin(jnp.pi * number * freq * freq / width))
    table_ref[:, :width] = matrix
    table_ref[:, width:] = matrix


def circ(number, width):
    return pl.pallas_call(
        circ_kernel,
        out_shape=jax.ShapeDtypeStruct((DEEP, 2 * width), BF16),
        in_specs=[whole(pltpu.SMEM)],
        out_specs=whole(),
        compiler_params=room(8 * MIB),
        cost_estimate=cost(2**24, 3 * MIB),
        name="circ",
    )(number)


def term_kernel(number_ref, me_ref, contrast_ref, table_ref, *out_refs):
    n_dist = len(out_refs)
    blk, width = contrast_ref.shape
    quarter = width // n_dist
    me = me_ref[0]
    value = jnp.full((16, quarter), number_ref[0], F32)
    for k, ref in enumerate(out_refs):
        at = (me ^ k) * quarter
        total = jnp.zeros((blk, quarter), F32)
        for i in range(width // DEEP):
            start = pl.multiple_of(lax.rem(width - i * DEEP + at, width), 128)
            total += jnp.dot(
                contrast_ref[:, i * DEEP : (i + 1) * DEEP],
                table_ref[:, pl.ds(start, quarter)],
                preferred_element_type=F32,
            )
        ref[:blk] = total.astype(BF16)
        if k:
            rest, parts = value, []
            for _ in range(3):
                parts.append(rest.astype(BF16).astype(F32))
                rest = rest - parts[-1]
            which = lax.broadcasted_iota(jnp.int32, value.shape, 0)
            packed = jnp.where(which == 0, parts[0], jnp.where(which == 1, parts[1], parts[2]))
            ref[blk:] = packed.astype(BF16)


def terms_of(number, me, contrast, table, n_dist):
    blk, width = contrast.shape
    quarter = width // n_dist
    return pl.pallas_call(
        term_kernel,
        out_shape=[
            jax.ShapeDtypeStruct((blk + (16 if k else 0), quarter), BF16) for k in range(n_dist)
        ],
        in_specs=[whole(pltpu.SMEM), whole(pltpu.SMEM), whole(), whole()],
        out_specs=[whole()] * n_dist,
        compiler_params=room(12 * MIB),
        cost_estimate=cost(2 * blk * width * width, 3 * MIB),
        name="terms",
    )(number, me, contrast, table)


def table_kernel(number_ref, *refs):
    term_refs, (table_ref, sum_ref) = refs[:-2], refs[-2:]
    blk, quarter = sum_ref.shape
    width = table_ref.shape[1] - quarter
    short, long = width // 128, 128
    freq = frequencies(short, long)
    total = term_refs[0][...].astype(F32)
    factor = jnp.sin(jnp.pi * jnp.full((short, long), number_ref[0], F32) * freq * freq / width)
    squares = factor * factor
    for ref in term_refs[1:]:
        total += ref[:blk].astype(F32)
        parts = ref[blk:, :long].astype(F32)
        number = (parts[0:1] + parts[1:2]) + parts[2:3]
        factor = jnp.sin(jnp.pi * jnp.broadcast_to(number, (short, long)) * freq * freq / width)
        squares += factor * factor
    sum_ref[...] = total
    matrix = circulant(4.0 * squares - 2.0 * len(term_refs))
    table_ref[:, :width] = matrix
    table_ref[:, width:] = matrix[:, :quarter]


def table_of(number, terms):
    n_dist = len(terms)
    blk, quarter = terms[0].shape
    width = n_dist * quarter
    return pl.pallas_call(
        table_kernel,
        out_shape=(
            jax.ShapeDtypeStruct((DEEP, width + quarter), BF16),
            jax.ShapeDtypeStruct((blk, quarter), F32),
        ),
        in_specs=[whole(pltpu.SMEM)] + [whole()] * n_dist,
        out_specs=[whole()] * 2,
        compiler_params=room(12 * MIB),
        cost_estimate=cost(2**24, 3 * MIB),
        name="table",
    )(number, *terms)


def filter_kernel(n_dist, first, me_ref, own_ref, term_ref, table_ref, *refs):
    parts, out_ref = refs[:n_dist], refs[-1]
    rows, quarter = own_ref.shape
    width = n_dist * quarter
    me = me_ref[0]
    total = (2.0 * n_dist) * own_ref[...] + term_ref[first : first + rows]
    for k, ref in enumerate(parts):
        for h in range(quarter // DEEP):
            start = (me - (me ^ k)) * quarter - h * DEEP + width
            start = pl.multiple_of(lax.rem(start, width), 128)
            total += jnp.dot(
                ref[:, h * DEEP : (h + 1) * DEEP],
                table_ref[:, pl.ds(start, quarter)],
                preferred_element_type=F32,
            )
    out_ref[...] = total.astype(BF16)


def filtered(me, own, term, table, parts, first):
    rows, quarter = own.shape
    n_dist = len(parts)
    return pl.pallas_call(
        functools.partial(filter_kernel, n_dist, first),
        out_shape=jax.ShapeDtypeStruct((rows, quarter), BF16),
        in_specs=[whole(pltpu.SMEM)] + [whole()] * (3 + n_dist),
        out_specs=whole(),
        compiler_params=room(4 * MIB),
        cost_estimate=cost(2 * rows * quarter * quarter * n_dist, 3 * MIB),
        name="filter",
    )(me, own, term, table, *parts)


def back_kernel(owners, me_ref, targets_ref, kernels_ref, *refs):
    parts, (out_hbm, chosen, out, sems) = refs[:-4], refs[-4:]
    vblocks, blk, _ = out.shape
    top = kernels_ref.shape[1]
    for c, (start, rows) in enumerate(chunks_of(blk)):
        for k in range(owners):
            chosen[k, start : start + rows] = parts[c * owners + k][...]
    me = me_ref[0]
    group = 4
    copies = []
    for step in range(vblocks // group):
        for b in range(step * group, (step + 1) * group):
            picked = [chosen[targets_ref[t, b] ^ me] for t in range(top)]
            out[b] = lax.dot_general(
                kernels_ref[b].reshape(top * blk, blk),
                jnp.concatenate(picked, axis=0),
                (((0,), (0,)), ((), ())),
                preferred_element_type=F32,
            ).astype(BF16)
        part = pl.ds(step * group, group)
        copies.append(pltpu.make_async_copy(out.at[part], out_hbm.at[part], sems.at[step]))
        copies[-1].start()
    for copy in copies:
        copy.wait()


def back(me, targets, kernels, parts, owners):
    vblocks, top, blk, _ = kernels.shape
    quarter = parts[0].shape[1]
    return pl.pallas_call(
        functools.partial(back_kernel, owners),
        out_shape=jax.ShapeDtypeStruct((vblocks, blk, quarter), BF16),
        in_specs=[whole(pltpu.SMEM)] * 2 + [whole()] * (1 + len(parts)),
        out_specs=whole(pltpu.HBM),
        scratch_shapes=[
            pltpu.VMEM((owners, blk, quarter), BF16),
            pltpu.VMEM((vblocks, blk, quarter), BF16),
            pltpu.SemaphoreType.DMA((vblocks,)),
        ],
        compiler_params=room(2 * (owners + vblocks) * blk * quarter + 6 * MIB),
        cost_estimate=cost(2 * vblocks * top * blk * blk * quarter, 4 * MIB),
        name="back",
    )(me, targets, kernels, *parts)


def shards(volume, kernels, targets, contrast, fresnel_numbers):
    owners, n_dist = lax.axis_size("rows"), lax.axis_size("dist")
    me_rows = lax.axis_index("rows").astype(jnp.int32).reshape(1)
    me_dist = lax.axis_index("dist").astype(jnp.int32).reshape(1)
    targets = targets.T

    send, keep = project(me_rows, targets, kernels, volume, owners)
    contrast_table = circ(fresnel_numbers, contrast.shape[-1])
    came = swap(send, "rows", 1)
    own, *outgoing = pair_sum(keep, came, 1)
    arrived = []
    for k, x in enumerate(outgoing):
        arrived.append(swap(x, "rows", 2 * (k + 1)))

    terms = terms_of(fresnel_numbers, me_dist, contrast[0, 0], contrast_table, n_dist)
    came = [terms[0]]
    for k in range(1, n_dist):
        came.append(swap(terms[k], "dist", k))
    table, term = table_of(fresnel_numbers, came)

    totals, rounded = total_sum(own, arrived)
    pieces = []
    for c, (start, _) in enumerate(chunks_of(own.shape[0])):
        total = totals[c]
        parts = [rounded[c]]
        for k in range(1, n_dist):
            parts.append(swap(rounded[c], "dist", k))
        image = filtered(me_dist, total, term, table, parts, start)
        found = [image]
        for rel in range(1, owners):
            low = rel & -rel
            found.append(swap(found[rel ^ low], "rows", low))
        pieces += found
    return back(me_rows, targets, kernels, pieces, owners)


def solution(mesh):
    in_specs = (
        P("rows", None, "dist"),
        P("rows", None, None, None),
        P("rows", None),
        P("dist", "rows", None, None),
        P("dist"),
    )
    out_specs = P("rows", None, "dist")

    return jax.shard_map(shards, mesh=mesh, in_specs=in_specs, out_specs=out_specs, check_vma=False)
```

time: 403 us -> 51.9 us (0.13); the launches traced: 398 us -> 51.8 us
  blocking collectives: 232 us -> 0 us
  matrix products: 74.9 us -> 0 us
  other arithmetic: 44.7 us -> 0 us
  starting transfers between devices: 0.26 us -> 24.2 us
  between operations: 14.4 us -> 0.8 us
  local copies, waits for them, and re-layouts: 11.7 us -> 0.02 us
  Pallas kernels: 0 us -> 9.95 us
    all_to_all x1 -> x0, blocking collectives: 191 us -> none  [shards(): lax.all_to_all(outgoing, 'rows', split_axis=0, concat_axis=0, tiled=True)]
    dot_general x8 -> x0, matrix products: 74.9 us -> none  [the longest x2 40.1 us: synthesize(): lax.dot_general(coeffs * weight, table, (((1,), (1,)), ((), ())), precisi...]
    psum x1 -> x0, blocking collectives: 41 us -> none  [shards(): summed = lax.psum(term, 'dist')]
    cos x1 -> x0, other arithmetic: 34.4 us -> none  [spectral_table(): return jnp.concatenate([jnp.cos(turns), jnp.sin(turns)], axis=1)]
    ppermute x0 -> x27, starting transfers between devices: none -> 24.2 us  [swap(): return lax.ppermute(x, axis, [(i, i ^ mask) for i in range(size)])]
    all_gather x2 -> x0, waiting for transfers between devices: 20.7 us -> none  [the longest x1 20.7 us: shards(): piece = lax.all_gather(image_gradient[None], 'rows', axis=0, tiled=True)]
    ppermute x0 -> x27, waiting for transfers between devices: none -> 16.8 us  [swap(): return lax.ppermute(x, axis, [(i, i ^ mask) for i in range(size)])]
    reduce_sum x3 -> x0, other arithmetic: 10.2 us -> none  [the longest x1 9.19 us: shards(): jnp.sum(arrived.astype(jnp.float32), axis=1).astype(jnp.bfloat16)]
  transfers between devices with their start and end apart: 2 -> 27, of which waited for: 1 -> 9; matrix products, arithmetic and copies ran while one was open for 9% -> 0% of each run, Pallas kernels for 0% -> 8%
where the time goes in v2:
time: 51.9 us; the launch traced here: 51.8 us
  starting transfers between devices  24.2 us (47%)
  waiting for transfers between devices  16.8 us (32%)
  Pallas kernels  9.95 us (19%)
  between operations  0.8 us (2%)
    ppermute x27, starting transfers between devices, swap(): return lax.ppermute(x, axis, [(i, i ^ mask) for i in range(size)])  24.2 us
    ppermute x27, waiting for transfers between devices, swap(): return lax.ppermute(x, axis, [(i, i ^ mask) for i in range(size)])  16.8 us
    pallas_call x1, Pallas kernels, project(): pl.pallas_call(project_kernel, out_shape=(out, out), in_specs=[whole(pltp...  3.19 us
    pallas_call x1, Pallas kernels, back(): pl.pallas_call(functools.partial(back_kernel, owners), out_shape=jax.Shap...  2.39 us
    pallas_call x1, Pallas kernels, terms_of(): pl.pallas_call(term_kernel, out_shape=[jax.ShapeDtypeStruct((blk + (16 if...  1.29 us
    pallas_call x1, Pallas kernels, table_of(): pl.pallas_call(table_kernel, out_shape=(jax.ShapeDtypeStruct((DEEP, width...  1.04 us
  transfers between devices with their start and end apart: 27, of which 9 were waited for; matrix products, arithmetic and copies ran while one was open for 0% of the time, Pallas kernels for 8%

profile of v2, /device:TPU:0, one launch (start us, length us, event | category | flops | bytes accessed | tf_op | source)
XLA Modules:
  0.0 51.8 jit_solution(3239986698374829445)
XLA Ops:
  0.0 3.2 %project.1 = (bf16[4,128,512]{2,1,0:T(8,128)(2,1)S(1)}, bf16[4,128,512]{2,1,0:T(8,128)(2,1)S(1)}) custom-call(s32[1]{0:T(128)} %bitcast.me_ref, s32[2,16]{1,0:T(2,128)} %bitcast.4, bf16[16,2,128,128]{3,2,1,0:T(8,128)(2,1)} %kernels_ref.1, bf16[16,128,512]{2,1,0:T(8,128)(2,1)} %refs_2_.1), custom_call_target="tpu_custom_call" | custom-call | flops 536870912 | bytes 4194304 | tf_op jit(solution)/shard_map/project/pallas_call | solution.py:91
  3.2 0.0 copy-start.2
  3.2 0.6 %collective-permute-start = (bf16[4,128,512]{2,1,0:T(8,128)(2,1)S(1)}, bf16[4,128,512]{2,1,0:T(8,128)(2,1)S(1)}, u32[]{:S(2)}, u32[]{:S(2)}) collective-permute-start(bf16[4,128,512]{2,1,0:T(8,128)(2,1)S(1)} %get-tuple-element.22), channel_id=1, source_target_pairs={{0,1},{1,0},{2,3},{3,2},{4,5},{5,4},{6,7},{7,6},{8,9},{9,8},{10,11... | collective-permute-start | bytes 1572872 | tf_op jit(solution)/shard_map/ppermute | solution.py:25
  3.8 1.5 %collective-permute-done.came_ref = bf16[4,128,512]{2,1,0:T(8,128)(2,1)S(1)} collective-permute-done((bf16[4,128,512]{2,1,0:T(8,128)(2,1)S(1)}, bf16[4,128,512]{2,1,0:T(8,128)(2,1)S(1)}, u32[]{:S(2)}, u32[]{:S(2)}) %collective-permute-start) | collective-permute-done | bytes 524320 | tf_op jit(solution)/shard_map/ppermute | solution.py:25
  5.3 0.1 pair_sum.1
  5.4 3.0 %collective-permute-start.1 = (bf16[128,512]{1,0:T(8,128)(2,1)S(1)}, bf16[128,512]{1,0:T(8,128)(2,1)S(1)}, u32[]{:S(2)}, u32[]{:S(2)}) collective-permute-start(bf16[128,512]{1,0:T(8,128)(2,1)S(1)} %get-tuple-element.24), channel_id=1, source_target_pairs={{0,2},{1,3},{2,0},{3,1},{4,6},{5,7},{6,4},{7,5},{8,10},{9,11},{10,... | collective-permute-start | bytes 393224 | tf_op jit(solution)/shard_map/ppermute | solution.py:25
  9.1 0.9 %circ.1.table_ref = bf16[256,4096]{1,0:T(8,128)(2,1)S(1)} custom-call(f32[1]{0:T(128)S(6)} %copy.6.number_ref), custom_call_target="tpu_custom_call" | custom-call | flops 16777216 | bytes 3145728 | tf_op jit(solution)/shard_map/circ/pallas_call | solution.py:206
  10.0 2.7 %collective-permute-start.2 = (bf16[128,512]{1,0:T(8,128)(2,1)S(1)}, bf16[128,512]{1,0:T(8,128)(2,1)S(1)}, u32[]{:S(2)}, u32[]{:S(2)}) collective-permute-start(bf16[128,512]{1,0:T(8,128)(2,1)S(1)} %get-tuple-element.25), channel_id=1, source_target_pairs={{0,4},{1,5},{2,6},{3,7},{4,0},{5,1},{6,2},{7,3},{8,12},{9,13},{10,... | collective-permute-start | bytes 393224 | tf_op jit(solution)/shard_map/ppermute | solution.py:25
  12.6 0.0 collective-permute-start.3
  12.6 1.3 %terms.1 = (bf16[128,512]{1,0:T(8,128)(2,1)S(1)}, bf16[144,512]{1,0:T(8,128)(2,1)S(1)}, bf16[144,512]{1,0:T(8,128)(2,1)S(1)}, bf16[144,512]{1,0:T(8,128)(2,1)S(1)}) custom-call(f32[1]{0:T(128)S(6)} %copy.6.number_ref, s32[1]{0:T(128)} %bitcast.2.me_ref, bf16[128,2048]{1,0:T(8,128)(2,1)S(1)} %bitcast.6, bf16[256,4096]{1,0:T(8,128)(2,1)S(1)} %circ.1.table_ref), custom_call_target="tpu_custom_call" | custom-call | flops 1073741824 | bytes 3145728 | tf_op jit(solution)/shard_map/terms/pallas_call | solution.py:247
  13.9 1.8 %collective-permute-start.4 = (bf16[144,512]{1,0:T(8,128)(2,1)S(1)}, bf16[144,512]{1,0:T(8,128)(2,1)S(1)}, u32[]{:S(2)}, u32[]{:S(2)}) collective-permute-start(bf16[144,512]{1,0:T(8,128)(2,1)S(1)} %get-tuple-element.29), channel_id=1, source_target_pairs={{0,8},{8,0},{16,24},{24,16},{1,9},{9,1},{17,25},{25,17},{2,10},{10... | collective-permute-start | bytes 442376 | tf_op jit(solution)/shard_map/ppermute | solution.py:25
  15.7 1.5 %collective-permute-start.5 = (bf16[144,512]{1,0:T(8,128)(2,1)S(1)}, bf16[144,512]{1,0:T(8,128)(2,1)S(1)}, u32[]{:S(2)}, u32[]{:S(2)}) collective-permute-start(bf16[144,512]{1,0:T(8,128)(2,1)S(1)} %get-tuple-element.30), channel_id=1, source_target_pairs={{0,16},{8,24},{16,0},{24,8},{1,17},{9,25},{17,1},{25,9},{2,18},{10... | collective-permute-start | bytes 442376 | tf_op jit(solution)/shard_map/ppermute | solution.py:25
  17.2 0.0 collective-permute-done.1.refs_0_
  17.2 0.3 collective-permute-start.6
  17.5 5.0 %collective-permute-done.2.refs_1_ = bf16[128,512]{1,0:T(8,128)(2,1)S(1)} collective-permute-done((bf16[128,512]{1,0:T(8,128)(2,1)S(1)}, bf16[128,512]{1,0:T(8,128)(2,1)S(1)}, u32[]{:S(2)}, u32[]{:S(2)}) %collective-permute-start.2) | collective-permute-done | bytes 131104 | tf_op jit(solution)/shard_map/ppermute | solution.py:25
  22.5 0.0 collective-permute-done.3.refs_2_
  22.5 0.1 total_sum.1
  22.5 1.6 %collective-permute-start.7 = (bf16[64,512]{1,0:T(8,128)(2,1)S(1)}, bf16[64,512]{1,0:T(8,128)(2,1)S(1)}, u32[]{:S(2)}, u32[]{:S(2)}) collective-permute-start(bf16[64,512]{1,0:T(8,128)(2,1)S(1)} %get-tuple-element.34.refs_0_), channel_id=1, source_target_pairs={{0,8},{8,0},{16,24},{24,16},{1,9},{9,1},{17,25},{25,17},{2,10},{10... | collective-permute-start | bytes 196616 | tf_op jit(solution)/shard_map/ppermute | solution.py:25
  24.1 1.5 %collective-permute-start.8 = (bf16[64,512]{1,0:T(8,128)(2,1)S(1)}, bf16[64,512]{1,0:T(8,128)(2,1)S(1)}, u32[]{:S(2)}, u32[]{:S(2)}) collective-permute-start(bf16[64,512]{1,0:T(8,128)(2,1)S(1)} %get-tuple-element.34.refs_0_), channel_id=1, source_target_pairs={{0,16},{8,24},{16,0},{24,8},{1,17},{9,25},{17,1},{25,9},{2,18},{10... | collective-permute-start | bytes 196616 | tf_op jit(solution)/shard_map/ppermute | solution.py:25
  25.6 0.0 collective-permute-done.4.refs_1_
  25.6 0.5 collective-permute-start.9
  26.1 0.0 collective-permute-done.5.refs_2_
  26.1 1.5 %collective-permute-start.17 = (bf16[64,512]{1,0:T(8,128)(2,1)S(1)}, bf16[64,512]{1,0:T(8,128)(2,1)S(1)}, u32[]{:S(2)}, u32[]{:S(2)}) collective-permute-start(bf16[64,512]{1,0:T(8,128)(2,1)S(1)} %get-tuple-element.36.refs_0_), channel_id=1, source_target_pairs={{0,8},{8,0},{16,24},{24,16},{1,9},{9,1},{17,25},{25,17},{2,10},{10... | collective-permute-start | bytes 196616 | tf_op jit(solution)/shard_map/ppermute | solution.py:25
  27.6 0.0 collective-permute-done.6.refs_3_
  27.6 1.5 %collective-permute-start.18 = (bf16[64,512]{1,0:T(8,128)(2,1)S(1)}, bf16[64,512]{1,0:T(8,128)(2,1)S(1)}, u32[]{:S(2)}, u32[]{:S(2)}) collective-permute-start(bf16[64,512]{1,0:T(8,128)(2,1)S(1)} %get-tuple-element.36.refs_0_), channel_id=1, source_target_pairs={{0,16},{8,24},{16,0},{24,8},{1,17},{9,25},{17,1},{25,9},{2,18},{10... | collective-permute-start | bytes 196616 | tf_op jit(solution)/shard_map/ppermute | solution.py:25
  29.1 0.0 collective-permute-done.7.refs_1_
  29.1 0.5 collective-permute-start.19
  29.6 1.0 %table.1 = (bf16[256,2560]{1,0:T(8,128)(2,1)S(1)}, f32[128,512]{1,0:T(8,128)S(1)}) custom-call(f32[1]{0:T(128)S(6)} %copy.6.number_ref, bf16[128,512]{1,0:T(8,128)(2,1)S(1)} %get-tuple-element.28.refs_0_, bf16[144,512]{1,0:T(8,128)(2,1)S(1)} %collective-permute-done.4.refs_1_, bf16[144,512]{1,0:T(8,128)(2,1)S(1)} %collective-permute-done.5.refs_2_, ...), custom_call_target="tpu_custom_call" | custom-call | flops 16777216 | bytes 3145728 | tf_op jit(solution)/shard_map/table/pallas_call | solution.py:285
  30.7 0.0 copy-start
  30.7 0.0 copy-start.1
  30.7 0.0 collective-permute-done.8.refs_2_
  30.7 0.8 %collective-permute-done.9.refs_3_ = bf16[64,512]{1,0:T(8,128)(2,1)S(1)} collective-permute-done((bf16[64,512]{1,0:T(8,128)(2,1)S(1)}, bf16[64,512]{1,0:T(8,128)(2,1)S(1)}, u32[]{:S(2)}, u32[]{:S(2)}) %collective-permute-start.9) | collective-permute-done | bytes 65568 | tf_op jit(solution)/shard_map/ppermute | solution.py:25
  31.5 0.5 filter.2.refs_0_
  31.9 0.1 collective-permute-start.10
  32.0 2.4 %collective-permute-start.11 = (bf16[64,512]{1,0:T(8,128)(2,1)S(1)}, bf16[64,512]{1,0:T(8,128)(2,1)S(1)}, u32[]{:S(2)}, u32[]{:S(2)}) collective-permute-start(bf16[64,512]{1,0:T(8,128)(2,1)S(1)} %filter.2.refs_0_), channel_id=1, source_target_pairs={{0,2},{1,3},{2,0},{3,1},{4,6},{5,7},{6,4},{7,5},{8,10},{9,11},{10,... | collective-permute-start | bytes 196616 | tf_op jit(solution)/shard_map/ppermute | solution.py:25
  34.5 0.0 collective-permute-done.17.refs_1_
  34.5 1.3 %collective-permute-start.13 = (bf16[64,512]{1,0:T(8,128)(2,1)S(1)}, bf16[64,512]{1,0:T(8,128)(2,1)S(1)}, u32[]{:S(2)}, u32[]{:S(2)}) collective-permute-start(bf16[64,512]{1,0:T(8,128)(2,1)S(1)} %filter.2.refs_0_), channel_id=1, source_target_pairs={{0,4},{1,5},{2,6},{3,7},{4,0},{5,1},{6,2},{7,3},{8,12},{9,13},{10,... | collective-permute-start | bytes 196616 | tf_op jit(solution)/shard_map/ppermute | solution.py:25
  35.8 0.0 collective-permute-done.18.refs_2_
  35.8 0.0 collective-permute-done.19.refs_3_
  35.8 0.5 filter.3.refs_8_
  36.3 2.3 %collective-permute-start.23 = (bf16[64,512]{1,0:T(8,128)(2,1)S(1)}, bf16[64,512]{1,0:T(8,128)(2,1)S(1)}, u32[]{:S(2)}, u32[]{:S(2)}) collective-permute-start(bf16[64,512]{1,0:T(8,128)(2,1)S(1)} %filter.3.refs_8_), channel_id=1, source_target_pairs={{0,4},{1,5},{2,6},{3,7},{4,0},{5,1},{6,2},{7,3},{8,12},{9,13},{10,... | collective-permute-start | bytes 196616 | tf_op jit(solution)/shard_map/ppermute | solution.py:25
  38.6 0.0 collective-permute-start.20
  38.6 0.0 collective-permute-done.10.refs_1_
  38.6 0.0 collective-permute-start.21
  38.6 0.0 collective-permute-done.11.refs_2_
  38.6 0.6 %collective-permute-start.12 = (bf16[64,512]{1,0:T(8,128)(2,1)S(1)}, bf16[64,512]{1,0:T(8,128)(2,1)S(1)}, u32[]{:S(2)}, u32[]{:S(2)}) collective-permute-start(bf16[64,512]{1,0:T(8,128)(2,1)S(1)} %collective-permute-done.11.refs_2_), channel_id=1, source_target_pairs={{0,1},{1,0},{2,3},{3,2},{4,5},{5,4},{6,7},{7,6},{8,9},{9,8},{10,11... | collective-permute-start | bytes 196616 | tf_op jit(solution)/shard_map/ppermute | solution.py:25
  39.2 2.8 %collective-permute-done.13.refs_4_ = bf16[64,512]{1,0:T(8,128)(2,1)S(1)} collective-permute-done((bf16[64,512]{1,0:T(8,128)(2,1)S(1)}, bf16[64,512]{1,0:T(8,128)(2,1)S(1)}, u32[]{:S(2)}, u32[]{:S(2)}) %collective-permute-start.13) | collective-permute-done | bytes 65568 | tf_op jit(solution)/shard_map/ppermute | solution.py:25
  42.0 0.0 collective-permute-start.15
  42.0 1.9 %collective-permute-done.23.refs_12_ = bf16[64,512]{1,0:T(8,128)(2,1)S(1)} collective-permute-done((bf16[64,512]{1,0:T(8,128)(2,1)S(1)}, bf16[64,512]{1,0:T(8,128)(2,1)S(1)}, u32[]{:S(2)}, u32[]{:S(2)}) %collective-permute-start.23) | collective-permute-done | bytes 65568 | tf_op jit(solution)/shard_map/ppermute | solution.py:25
  43.9 0.2 collective-permute-start.25
  44.0 0.0 collective-permute-done.20.refs_9_
  44.0 0.0 collective-permute-start.14
  44.0 0.6 %collective-permute-done.21.refs_10_ = bf16[64,512]{1,0:T(8,128)(2,1)S(1)} collective-permute-done((bf16[64,512]{1,0:T(8,128)(2,1)S(1)}, bf16[64,512]{1,0:T(8,128)(2,1)S(1)}, u32[]{:S(2)}, u32[]{:S(2)}) %collective-permute-start.21) | collective-permute-done | bytes 65568 | tf_op jit(solution)/shard_map/ppermute | solution.py:25
  44.6 0.0 collective-permute-start.24
  44.7 0.0 collective-permute-done.12.refs_3_
  44.7 0.5 collective-permute-start.22
  45.2 1.1 %collective-permute-done.15.refs_6_ = bf16[64,512]{1,0:T(8,128)(2,1)S(1)} collective-permute-done((bf16[64,512]{1,0:T(8,128)(2,1)S(1)}, bf16[64,512]{1,0:T(8,128)(2,1)S(1)}, u32[]{:S(2)}, u32[]{:S(2)}) %collective-permute-start.15) | collective-permute-done | bytes 65568 | tf_op jit(solution)/shard_map/ppermute | solution.py:25
  46.3 1.9 %collective-permute-done.25.refs_14_ = bf16[64,512]{1,0:T(8,128)(2,1)S(1)} collective-permute-done((bf16[64,512]{1,0:T(8,128)(2,1)S(1)}, bf16[64,512]{1,0:T(8,128)(2,1)S(1)}, u32[]{:S(2)}, u32[]{:S(2)}) %collective-permute-start.25) | collective-permute-done | bytes 65568 | tf_op jit(solution)/shard_map/ppermute | solution.py:25
  48.1 0.0 collective-permute-start.26
  48.1 0.0 collective-permute-done.14.refs_5_
  48.1 0.0 collective-permute-done.22.refs_11_
  48.1 0.0 collective-permute-done.16.refs_7_
  48.2 1.2 %collective-permute-done.26.refs_15_ = bf16[64,512]{1,0:T(8,128)(2,1)S(1)} collective-permute-done((bf16[64,512]{1,0:T(8,128)(2,1)S(1)}, bf16[64,512]{1,0:T(8,128)(2,1)S(1)}, u32[]{:S(2)}, u32[]{:S(2)}) %collective-permute-start.26) | collective-permute-done | bytes 65568 | tf_op jit(solution)/shard_map/ppermute | solution.py:25
  49.4 2.4 %back.1 = bf16[16,128,512]{2,1,0:T(8,128)(2,1)} custom-call(s32[1]{0:T(128)} %bitcast.me_ref, s32[2,16]{1,0:T(2,128)S(1)} %bitcast.5, bf16[16,2,128,128]{3,2,1,0:T(8,128)(2,1)S(1)} %copy-done, bf16[64,512]{1,0:T(8,128)(2,1)S(1)} %filter.2.refs_0_, bf16[64,512]{1,0:T(8,128)(2,1)S(1)} %collective-permute-done.10.refs_1_, ...), custom_call_target="tpu_custom_call" | custom-call | flops 536870912 | bytes 4194304 | tf_op jit(solution)/shard_map/back/pallas_call | solution.py:360
  (5 shorter events, 0.0 us)
Async XLA Ops:
  3.2 9.4 %copy-start.2 = (bf16[1,1,128,2048]{3,2,1,0:T(8,128)(2,1)S(1)}, bf16[1,1,128,2048]{3,2,1,0:T(8,128)(2,1)}, u32[]{:S(2)}) copy-start(bf16[1,1,128,2048]{3,2,1,0:T(8,128)(2,1)} %param.8) | copy-start | bytes 1572868
  3.2 2.1 %collective-permute-start = (bf16[4,128,512]{2,1,0:T(8,128)(2,1)S(1)}, bf16[4,128,512]{2,1,0:T(8,128)(2,1)S(1)}, u32[]{:S(2)}, u32[]{:S(2)}) collective-permute-start(bf16[4,128,512]{2,1,0:T(8,128)(2,1)S(1)} %get-tuple-element.22), channel_id=1, source_target_pairs={{0,1},{1,0},{2,3},{3,2},{4,5},{5,4},{6,7},{7,6},{8,9},{9,8},{10,11... | collective-permute-start | bytes 1572872 | tf_op jit(solution)/shard_map/ppermute | solution.py:25
  5.4 11.8 %collective-permute-start.1 = (bf16[128,512]{1,0:T(8,128)(2,1)S(1)}, bf16[128,512]{1,0:T(8,128)(2,1)S(1)}, u32[]{:S(2)}, u32[]{:S(2)}) collective-permute-start(bf16[128,512]{1,0:T(8,128)(2,1)S(1)} %get-tuple-element.24), channel_id=1, source_target_pairs={{0,2},{1,3},{2,0},{3,1},{4,6},{5,7},{6,4},{7,5},{8,10},{9,11},{10,... | collective-permute-start | bytes 393224 | tf_op jit(solution)/shard_map/ppermute | solution.py:25
  10.0 12.5 %collective-permute-start.2 = (bf16[128,512]{1,0:T(8,128)(2,1)S(1)}, bf16[128,512]{1,0:T(8,128)(2,1)S(1)}, u32[]{:S(2)}, u32[]{:S(2)}) collective-permute-start(bf16[128,512]{1,0:T(8,128)(2,1)S(1)} %get-tuple-element.25), channel_id=1, source_target_pairs={{0,4},{1,5},{2,6},{3,7},{4,0},{5,1},{6,2},{7,3},{8,12},{9,13},{10,... | collective-permute-start | bytes 393224 | tf_op jit(solution)/shard_map/ppermute | solution.py:25
  12.6 9.8 %collective-permute-start.3 = (bf16[128,512]{1,0:T(8,128)(2,1)S(1)}, bf16[128,512]{1,0:T(8,128)(2,1)S(1)}, u32[]{:S(2)}, u32[]{:S(2)}) collective-permute-start(bf16[128,512]{1,0:T(8,128)(2,1)S(1)} %get-tuple-element.26), channel_id=1, source_target_pairs={{0,6},{1,7},{2,4},{3,5},{4,2},{5,3},{6,0},{7,1},{8,14},{9,15},{10,... | collective-permute-start | bytes 393224 | tf_op jit(solution)/shard_map/ppermute | solution.py:25
  13.9 11.7 %collective-permute-start.4 = (bf16[144,512]{1,0:T(8,128)(2,1)S(1)}, bf16[144,512]{1,0:T(8,128)(2,1)S(1)}, u32[]{:S(2)}, u32[]{:S(2)}) collective-permute-start(bf16[144,512]{1,0:T(8,128)(2,1)S(1)} %get-tuple-element.29), channel_id=1, source_target_pairs={{0,8},{8,0},{16,24},{24,16},{1,9},{9,1},{17,25},{25,17},{2,10},{10... | collective-permute-start | bytes 442376 | tf_op jit(solution)/shard_map/ppermute | solution.py:25
  15.7 10.4 %collective-permute-start.5 = (bf16[144,512]{1,0:T(8,128)(2,1)S(1)}, bf16[144,512]{1,0:T(8,128)(2,1)S(1)}, u32[]{:S(2)}, u32[]{:S(2)}) collective-permute-start(bf16[144,512]{1,0:T(8,128)(2,1)S(1)} %get-tuple-element.30), channel_id=1, source_target_pairs={{0,16},{8,24},{16,0},{24,8},{1,17},{9,25},{17,1},{25,9},{2,18},{10... | collective-permute-start | bytes 442376 | tf_op jit(solution)/shard_map/ppermute | solution.py:25
  17.2 10.4 %collective-permute-start.6 = (bf16[144,512]{1,0:T(8,128)(2,1)S(1)}, bf16[144,512]{1,0:T(8,128)(2,1)S(1)}, u32[]{:S(2)}, u32[]{:S(2)}) collective-permute-start(bf16[144,512]{1,0:T(8,128)(2,1)S(1)} %get-tuple-element.31), channel_id=1, source_target_pairs={{0,24},{8,16},{16,8},{24,0},{1,25},{9,17},{17,9},{25,1},{2,26},{10... | collective-permute-start | bytes 442376 | tf_op jit(solution)/shard_map/ppermute | solution.py:25
  22.5 6.6 %collective-permute-start.7 = (bf16[64,512]{1,0:T(8,128)(2,1)S(1)}, bf16[64,512]{1,0:T(8,128)(2,1)S(1)}, u32[]{:S(2)}, u32[]{:S(2)}) collective-permute-start(bf16[64,512]{1,0:T(8,128)(2,1)S(1)} %get-tuple-element.34.refs_0_), channel_id=1, source_target_pairs={{0,8},{8,0},{16,24},{24,16},{1,9},{9,1},{17,25},{25,17},{2,10},{10... | collective-permute-start | bytes 196616 | tf_op jit(solution)/shard_map/ppermute | solution.py:25
  24.1 6.6 %collective-permute-start.8 = (bf16[64,512]{1,0:T(8,128)(2,1)S(1)}, bf16[64,512]{1,0:T(8,128)(2,1)S(1)}, u32[]{:S(2)}, u32[]{:S(2)}) collective-permute-start(bf16[64,512]{1,0:T(8,128)(2,1)S(1)} %get-tuple-element.34.refs_0_), channel_id=1, source_target_pairs={{0,16},{8,24},{16,0},{24,8},{1,17},{9,25},{17,1},{25,9},{2,18},{10... | collective-permute-start | bytes 196616 | tf_op jit(solution)/shard_map/ppermute | solution.py:25
  25.6 5.8 %collective-permute-start.9 = (bf16[64,512]{1,0:T(8,128)(2,1)S(1)}, bf16[64,512]{1,0:T(8,128)(2,1)S(1)}, u32[]{:S(2)}, u32[]{:S(2)}) collective-permute-start(bf16[64,512]{1,0:T(8,128)(2,1)S(1)} %get-tuple-element.34.refs_0_), channel_id=1, source_target_pairs={{0,24},{8,16},{16,8},{24,0},{1,25},{9,17},{17,9},{25,1},{2,26},{10... | collective-permute-start | bytes 196616 | tf_op jit(solution)/shard_map/ppermute | solution.py:25
  26.1 8.4 %collective-permute-start.17 = (bf16[64,512]{1,0:T(8,128)(2,1)S(1)}, bf16[64,512]{1,0:T(8,128)(2,1)S(1)}, u32[]{:S(2)}, u32[]{:S(2)}) collective-permute-start(bf16[64,512]{1,0:T(8,128)(2,1)S(1)} %get-tuple-element.36.refs_0_), channel_id=1, source_target_pairs={{0,8},{8,0},{16,24},{24,16},{1,9},{9,1},{17,25},{25,17},{2,10},{10... | collective-permute-start | bytes 196616 | tf_op jit(solution)/shard_map/ppermute | solution.py:25
  27.6 8.2 %collective-permute-start.18 = (bf16[64,512]{1,0:T(8,128)(2,1)S(1)}, bf16[64,512]{1,0:T(8,128)(2,1)S(1)}, u32[]{:S(2)}, u32[]{:S(2)}) collective-permute-start(bf16[64,512]{1,0:T(8,128)(2,1)S(1)} %get-tuple-element.36.refs_0_), channel_id=1, source_target_pairs={{0,16},{8,24},{16,0},{24,8},{1,17},{9,25},{17,1},{25,9},{2,18},{10... | collective-permute-start | bytes 196616 | tf_op jit(solution)/shard_map/ppermute | solution.py:25
  29.1 6.7 %collective-permute-start.19 = (bf16[64,512]{1,0:T(8,128)(2,1)S(1)}, bf16[64,512]{1,0:T(8,128)(2,1)S(1)}, u32[]{:S(2)}, u32[]{:S(2)}) collective-permute-start(bf16[64,512]{1,0:T(8,128)(2,1)S(1)} %get-tuple-element.36.refs_0_), channel_id=1, source_target_pairs={{0,24},{8,16},{16,8},{24,0},{1,25},{9,17},{17,9},{25,1},{2,26},{10... | collective-permute-start | bytes 196616 | tf_op jit(solution)/shard_map/ppermute | solution.py:25
  30.7 18.7 %copy-start = (bf16[16,2,128,128]{3,2,1,0:T(8,128)(2,1)S(1)}, bf16[16,2,128,128]{3,2,1,0:T(8,128)(2,1)}, u32[]{:S(2)}) copy-start(bf16[16,2,128,128]{3,2,1,0:T(8,128)(2,1)} %kernels_ref.1) | copy-start | bytes 3145732
  30.7 18.7 %copy-start.1 = (s32[16,2]{0,1:T(2,128)S(1)}, s32[16,2]{0,1:T(2,128)}, u32[]{:S(2)}) copy-start(s32[16,2]{0,1:T(2,128)} %param.7) | copy-start | bytes 388
  31.9 6.7 %collective-permute-start.10 = (bf16[64,512]{1,0:T(8,128)(2,1)S(1)}, bf16[64,512]{1,0:T(8,128)(2,1)S(1)}, u32[]{:S(2)}, u32[]{:S(2)}) collective-permute-start(bf16[64,512]{1,0:T(8,128)(2,1)S(1)} %filter.2.refs_0_), channel_id=1, source_target_pairs={{0,1},{1,0},{2,3},{3,2},{4,5},{5,4},{6,7},{7,6},{8,9},{9,8},{10,11... | collective-permute-start | bytes 196616 | tf_op jit(solution)/shard_map/ppermute | solution.py:25
  32.0 6.6 %collective-permute-start.11 = (bf16[64,512]{1,0:T(8,128)(2,1)S(1)}, bf16[64,512]{1,0:T(8,128)(2,1)S(1)}, u32[]{:S(2)}, u32[]{:S(2)}) collective-permute-start(bf16[64,512]{1,0:T(8,128)(2,1)S(1)} %filter.2.refs_0_), channel_id=1, source_target_pairs={{0,2},{1,3},{2,0},{3,1},{4,6},{5,7},{6,4},{7,5},{8,10},{9,11},{10,... | collective-permute-start | bytes 196616 | tf_op jit(solution)/shard_map/ppermute | solution.py:25
  34.5 7.5 %collective-permute-start.13 = (bf16[64,512]{1,0:T(8,128)(2,1)S(1)}, bf16[64,512]{1,0:T(8,128)(2,1)S(1)}, u32[]{:S(2)}, u32[]{:S(2)}) collective-permute-start(bf16[64,512]{1,0:T(8,128)(2,1)S(1)} %filter.2.refs_0_), channel_id=1, source_target_pairs={{0,4},{1,5},{2,6},{3,7},{4,0},{5,1},{6,2},{7,3},{8,12},{9,13},{10,... | collective-permute-start | bytes 196616 | tf_op jit(solution)/shard_map/ppermute | solution.py:25
  36.3 7.6 %collective-permute-start.23 = (bf16[64,512]{1,0:T(8,128)(2,1)S(1)}, bf16[64,512]{1,0:T(8,128)(2,1)S(1)}, u32[]{:S(2)}, u32[]{:S(2)}) collective-permute-start(bf16[64,512]{1,0:T(8,128)(2,1)S(1)} %filter.3.refs_8_), channel_id=1, source_target_pairs={{0,4},{1,5},{2,6},{3,7},{4,0},{5,1},{6,2},{7,3},{8,12},{9,13},{10,... | collective-permute-start | bytes 196616 | tf_op jit(solution)/shard_map/ppermute | solution.py:25
  38.6 5.4 %collective-permute-start.20 = (bf16[64,512]{1,0:T(8,128)(2,1)S(1)}, bf16[64,512]{1,0:T(8,128)(2,1)S(1)}, u32[]{:S(2)}, u32[]{:S(2)}) collective-permute-start(bf16[64,512]{1,0:T(8,128)(2,1)S(1)} %filter.3.refs_8_), channel_id=1, source_target_pairs={{0,1},{1,0},{2,3},{3,2},{4,5},{5,4},{6,7},{7,6},{8,9},{9,8},{10,11... | collective-permute-start | bytes 196616 | tf_op jit(solution)/shard_map/ppermute | solution.py:25
  38.6 6.0 %collective-permute-start.21 = (bf16[64,512]{1,0:T(8,128)(2,1)S(1)}, bf16[64,512]{1,0:T(8,128)(2,1)S(1)}, u32[]{:S(2)}, u32[]{:S(2)}) collective-permute-start(bf16[64,512]{1,0:T(8,128)(2,1)S(1)} %filter.3.refs_8_), channel_id=1, source_target_pairs={{0,2},{1,3},{2,0},{3,1},{4,6},{5,7},{6,4},{7,5},{8,10},{9,11},{10,... | collective-permute-start | bytes 196616 | tf_op jit(solution)/shard_map/ppermute | solution.py:25
  38.6 6.0 %collective-permute-start.12 = (bf16[64,512]{1,0:T(8,128)(2,1)S(1)}, bf16[64,512]{1,0:T(8,128)(2,1)S(1)}, u32[]{:S(2)}, u32[]{:S(2)}) collective-permute-start(bf16[64,512]{1,0:T(8,128)(2,1)S(1)} %collective-permute-done.11.refs_2_), channel_id=1, source_target_pairs={{0,1},{1,0},{2,3},{3,2},{4,5},{5,4},{6,7},{7,6},{8,9},{9,8},{10,11... | collective-permute-start | bytes 196616 | tf_op jit(solution)/shard_map/ppermute | solution.py:25
  42.0 4.3 %collective-permute-start.15 = (bf16[64,512]{1,0:T(8,128)(2,1)S(1)}, bf16[64,512]{1,0:T(8,128)(2,1)S(1)}, u32[]{:S(2)}, u32[]{:S(2)}) collective-permute-start(bf16[64,512]{1,0:T(8,128)(2,1)S(1)} %collective-permute-done.13.refs_4_), channel_id=1, source_target_pairs={{0,2},{1,3},{2,0},{3,1},{4,6},{5,7},{6,4},{7,5},{8,10},{9,11},{10,... | collective-permute-start | bytes 196616 | tf_op jit(solution)/shard_map/ppermute | solution.py:25
  43.9 4.3 %collective-permute-start.25 = (bf16[64,512]{1,0:T(8,128)(2,1)S(1)}, bf16[64,512]{1,0:T(8,128)(2,1)S(1)}, u32[]{:S(2)}, u32[]{:S(2)}) collective-permute-start(bf16[64,512]{1,0:T(8,128)(2,1)S(1)} %collective-permute-done.23.refs_12_), channel_id=1, source_target_pairs={{0,2},{1,3},{2,0},{3,1},{4,6},{5,7},{6,4},{7,5},{8,10},{9,11},{10,... | collective-permute-start | bytes 196616 | tf_op jit(solution)/shard_map/ppermute | solution.py:25
  44.0 4.1 %collective-permute-start.14 = (bf16[64,512]{1,0:T(8,128)(2,1)S(1)}, bf16[64,512]{1,0:T(8,128)(2,1)S(1)}, u32[]{:S(2)}, u32[]{:S(2)}) collective-permute-start(bf16[64,512]{1,0:T(8,128)(2,1)S(1)} %collective-permute-done.13.refs_4_), channel_id=1, source_target_pairs={{0,1},{1,0},{2,3},{3,2},{4,5},{5,4},{6,7},{7,6},{8,9},{9,8},{10,11... | collective-permute-start | bytes 196616 | tf_op jit(solution)/shard_map/ppermute | solution.py:25
  44.6 3.5 %collective-permute-start.24 = (bf16[64,512]{1,0:T(8,128)(2,1)S(1)}, bf16[64,512]{1,0:T(8,128)(2,1)S(1)}, u32[]{:S(2)}, u32[]{:S(2)}) collective-permute-start(bf16[64,512]{1,0:T(8,128)(2,1)S(1)} %collective-permute-done.23.refs_12_), channel_id=1, source_target_pairs={{0,1},{1,0},{2,3},{3,2},{4,5},{5,4},{6,7},{7,6},{8,9},{9,8},{10,11... | collective-permute-start | bytes 196616 | tf_op jit(solution)/shard_map/ppermute | solution.py:25
  44.7 3.5 %collective-permute-start.22 = (bf16[64,512]{1,0:T(8,128)(2,1)S(1)}, bf16[64,512]{1,0:T(8,128)(2,1)S(1)}, u32[]{:S(2)}, u32[]{:S(2)}) collective-permute-start(bf16[64,512]{1,0:T(8,128)(2,1)S(1)} %collective-permute-done.21.refs_10_), channel_id=1, source_target_pairs={{0,1},{1,0},{2,3},{3,2},{4,5},{5,4},{6,7},{7,6},{8,9},{9,8},{10,11... | collective-permute-start | bytes 196616 | tf_op jit(solution)/shard_map/ppermute | solution.py:25
  46.3 1.9 %collective-permute-start.16 = (bf16[64,512]{1,0:T(8,128)(2,1)S(1)}, bf16[64,512]{1,0:T(8,128)(2,1)S(1)}, u32[]{:S(2)}, u32[]{:S(2)}) collective-permute-start(bf16[64,512]{1,0:T(8,128)(2,1)S(1)} %collective-permute-done.15.refs_6_), channel_id=1, source_target_pairs={{0,1},{1,0},{2,3},{3,2},{4,5},{5,4},{6,7},{7,6},{8,9},{9,8},{10,11... | collective-permute-start | bytes 196616 | tf_op jit(solution)/shard_map/ppermute | solution.py:25
  48.1 1.3 %collective-permute-start.26 = (bf16[64,512]{1,0:T(8,128)(2,1)S(1)}, bf16[64,512]{1,0:T(8,128)(2,1)S(1)}, u32[]{:S(2)}, u32[]{:S(2)}) collective-permute-start(bf16[64,512]{1,0:T(8,128)(2,1)S(1)} %collective-permute-done.25.refs_14_), channel_id=1, source_target_pairs={{0,1},{1,0},{2,3},{3,2},{4,5},{5,4},{6,7},{7,6},{8,9},{9,8},{10,11... | collective-permute-start | bytes 196616 | tf_op jit(solution)/shard_map/ppermute | solution.py:25
